TPU v7x, 512 devices: a whole 4x8x8 slice. The times are simulated.
512 devices in a mesh: tok: 64 (over z, y_lo, core), head: 8 (over y_hi, x).
Axes of the slice: x: 4, y: 8 (y_hi: 2, y_lo: 4; y = y_hi * 4 + y_lo), z: 8, core: 2. Of those that a mesh axis runs over, the one named last changes fastest.
Arguments:
- queries: bfloat16 [16384, 2560], P('tok', 'head'), may hold values from -256 to 256
- keys: bfloat16 [16384, 2560], P('tok', 'head'), may hold values from -6 to 6
- values: bfloat16 [16384, 2560], P('tok', 'head'), may hold values from -6 to 6
- rates: float32 [16384, 8], P('tok', 'head'), may hold values from 0.00015625 to 0.003125
- back: int32 [16384], P('tok'), may hold values from 64 to 511
- group_end: int32 [1], replicated, may hold values from 4096 to 12287
- gate_init: float32 [8, 320, 320], P('head', None, 'tok'), may hold values from -0.3125 to 0.3125
- up_init: float32 [8, 320, 320], P('head', None, 'tok'), may hold values from -0.3125 to 0.3125
- down_init: float32 [8, 320, 320], P('head', None, 'tok'), may hold values from -0.3125 to 0.3125
- gain: float32 [2560], P('head'), may hold values from 0.5 to 1.5
Outputs:
- output: bfloat16 [16384, 2560], P('tok', 'head')
- gate_final: float32 [8, 320, 320], P('head', None, 'tok')
- up_final: float32 [8, 320, 320], P('head', None, 'tok')
- down_final: float32 [8, 320, 320], P('head', None, 'tok')
All inputs are finite; a program needn't handle non-finite values.
Results may differ from a plain program's by a relative error of at most 0.0088.
Values may be sent and summed in bfloat16 or wider, within the bound.
A program may use at most 64 MiB of HBM per device.

v0:
```python
import math

import jax
import jax.numpy as jnp
from jax import lax
from jax.sharding import PartitionSpec as P

HEADS = 8
HD = 320
WINDOW = 512


def shifted(value, axis, steps):
    count = lax.axis_size(axis)
    first, last = (max(0, -steps), min(count, count - steps))
    return lax.ppermute(value, axis, [(source, source + steps) for source in range(first, last)])


def from_everyone(array, axis):
    peers = lax.axis_size(axis)
    return lax.all_to_all(
        jnp.broadcast_to(array[None], (peers, *array.shape)), axis, 0, 0, tiled=True
    )


def joined_along(parts, dim):
    lengths = list(parts.shape[1:])
    lengths[dim] *= parts.shape[0]
    return jnp.moveaxis(parts, 0, dim).reshape(lengths)


def gathered_copies(array, axis, dim):
    parts = from_everyone(array, axis)
    return joined_along(parts, dim)


def split_up(array, dim, peers):
    before, after = (array.shape[:dim], array.shape[dim + 1 :])
    return jnp.moveaxis(array.reshape(*before, peers, -1, *after), dim, 0)


def sum_at_owner(array, axis, dim):
    parts = split_up(array, dim, lax.axis_size(axis))
    arrived = lax.all_to_all(parts, axis, split_axis=0, concat_axis=0, tiled=True)
    return arrived.sum(axis=0)


def of_everyone(array, axis):
    everything = from_everyone(array, axis)
    return jnp.sum(everything, axis=0)


def swiglu_apply(packed, inputs):
    pre_gate = jnp.einsum("thd,hdf->thf", inputs, packed[0], preferred_element_type=jnp.float32)
    pre_up = jnp.einsum("thd,hdf->thf", inputs, packed[1], preferred_element_type=jnp.float32)
    hidden = (pre_gate * jax.nn.sigmoid(pre_gate) * pre_up).astype(jnp.bfloat16)
    return jnp.einsum("thf,hfd->thd", hidden, packed[2], preferred_element_type=jnp.float32)


def swiglu_grads(packed, key_rows, value_rows, step_rates):
    pre_gate = jnp.einsum("thd,hdf->thf", key_rows, packed[0], preferred_element_type=jnp.float32)
    pre_up = jnp.einsum("thd,hdf->thf", key_rows, packed[1], preferred_element_type=jnp.float32)
    sigma = jax.nn.sigmoid(pre_gate)
    active = pre_gate * sigma
    hidden = (active * pre_up).astype(jnp.bfloat16)
    errors = (-step_rates[:, :, None] * value_rows).astype(jnp.bfloat16)
    grad_down = jnp.einsum("thf,thd->hfd", hidden, errors, preferred_element_type=jnp.float32)
    d_hidden = jnp.einsum("thd,hfd->thf", errors, packed[2], preferred_element_type=jnp.float32)
    d_gate = (d_hidden * pre_up * sigma * (1.0 + pre_gate * (1.0 - sigma))).astype(jnp.bfloat16)
    d_up = (d_hidden * active).astype(jnp.bfloat16)
    grad_gate = jnp.einsum("thd,thf->hdf", key_rows, d_gate, preferred_element_type=jnp.float32)
    grad_up = jnp.einsum("thd,thf->hdf", key_rows, d_up, preferred_element_type=jnp.float32)
    return (grad_gate, grad_up, grad_down)


def rescale(weight, grad):
    fresh = weight - grad
    old_norm = jnp.sqrt(jnp.sum(weight * weight, axis=1, keepdims=True))
    new_norm = jnp.sqrt(jnp.sum(fresh * fresh, axis=1, keepdims=True) + 1e-06)
    return fresh * (old_norm / new_norm)


def to_half(state):
    return tuple((w.astype(jnp.bfloat16) for w in state))


def unstack(stacked):
    return (stacked[0], stacked[1], stacked[2])


def fetch_tail(tails, distance):
    return shifted((tails[0], tails[1]), "tok", distance)


def on_device(queries, keys, values, rates, back, group_end, gate_init, up_init, down_init, gain):
    rows, heads = rates.shape
    width = queries.shape[1] // heads
    start = lax.axis_index("tok") * rows
    positions = start + jnp.arange(rows, dtype=jnp.int32)
    first = positions < group_end[0]
    query3 = queries.reshape(rows, heads, width)
    key3 = keys.reshape(rows, heads, width)
    value3 = values.reshape(rows, heads, width)
    rate_first = jnp.where(first[:, None], rates, 0.0)
    rate_second = jnp.where(first[:, None], 0.0, rates)
    group_list = ((rate_first, jnp.any(first)), (rate_second, jnp.logical_not(jnp.all(first))))
    empty_out = jnp.zeros((rows, heads, width), jnp.float32)

    def group_work(packed, step_rates, live):
        mixed = lax.cond(live, lambda: swiglu_apply(packed, query3), lambda: empty_out)
        shapes = tuple((jnp.zeros(w.shape, jnp.float32) for w in packed))
        grads = lax.cond(
            live, lambda: swiglu_grads(packed, key3, value3, step_rates), lambda: shapes
        )
        return (mixed, grads)

    outs = []
    shares = (gate_init, up_init, down_init)
    packed = unstack(gathered_copies(jnp.stack(to_half(shares)), "tok", 3))
    for number in range(2):
        step_rates, live = group_list[number]
        if number == 1:
            packed = unstack(gathered_copies(jnp.stack(to_half(shares)), "tok", 3))
        mixed, grads = group_work(packed, step_rates, live)
        outs.append(mixed)
        parts = unstack(sum_at_owner(jnp.stack(grads), "tok", 3))
        shares = tuple((rescale(w, g) for w, g in zip(shares, parts)))
    mixed = jnp.where(first[:, None, None], outs[0], outs[1])
    squares = of_everyone(jnp.sum(mixed * mixed, axis=(1, 2)), "head")
    mean_square = squares / (HEADS * HD)
    normed = mixed / jnp.sqrt(mean_square + 1e-06)[:, None, None] * gain.reshape(1, heads, width)
    reach_count = max(1, WINDOW // rows)
    tails = (keys, values)
    key_parts = []
    value_parts = []
    for distance in range(reach_count, 0, -1):
        prev_keys, prev_values = fetch_tail(tails, distance)
        key_parts.append(prev_keys)
        value_parts.append(prev_values)
    key_ext = jnp.concatenate(key_parts + [keys], axis=0).reshape(rows + WINDOW, heads, width)
    value_ext = jnp.concatenate(value_parts + [values], axis=0).reshape(rows + WINDOW, heads, width)
    block = math.gcd(rows, 512)
    scale = 1.0 / math.sqrt(width)
    number = 0
    begin = number * block
    q_pos = start + begin + jnp.arange(block, dtype=jnp.int32)
    k_pos = start + begin - WINDOW + jnp.arange(block + WINDOW, dtype=jnp.int32)
    allowed = (
        (k_pos[None, :] >= 0)
        & (k_pos[None, :] <= q_pos[:, None])
        & (k_pos[None, :] >= q_pos[:, None] - back[:, None])
    )
    scores = jnp.einsum("qhd,khd->hqk", query3, key_ext, preferred_element_type=jnp.float32) * scale
    scores = jnp.where(allowed[None], scores, -jnp.inf)
    top = jnp.max(scores, axis=2, keepdims=True)
    weights = jnp.where(allowed[None], jnp.exp(scores - top), 0.0)
    total = jnp.sum(weights, axis=2, keepdims=True)
    probs = (weights / total).astype(jnp.bfloat16)
    pieces = jnp.einsum("hqk,khd->qhd", probs, value_ext, preferred_element_type=jnp.float32)
    output = (normed + pieces).astype(jnp.bfloat16).reshape(rows, heads * width)
    return (output, shares[0], shares[1], shares[2])


def solution(mesh):
    placed = (
        P("tok", "head"),
        P("tok", "head"),
        P("tok", "head"),
        P("tok", "head"),
        P("tok"),
        P(),
        P("head", None, "tok"),
        P("head", None, "tok"),
        P("head", None, "tok"),
        P("head"),
    )
    return jax.shard_map(
        on_device,
        mesh=mesh,
        in_specs=placed,
        out_specs=(
            P("tok", "head"),
            P("head", None, "tok"),
            P("head", None, "tok"),
            P("head", None, "tok"),
        ),
        check_vma=False,
    )
```

profile of v0, /device:TPU:1, one launch (start us, length us, event | category | flops | bytes accessed | tf_op | source)
XLA Modules:
  0.0 218.0 jit_solution(392514345101637373)
XLA Ops:
  0.6 0.9 multiply_reduce_fusion.10
  1.5 0.7 fusion.98
  2.3 1.2 broadcast_in_dim.44
  3.5 15.4 %all-to-all-start = ((bf16[64,3,1,320,5]{3,1,4,2,0:T(4,128)(2,1)}), bf16[64,3,1,320,5]{3,1,4,2,0:T(4,128)(2,1)S(1)}, u32[]{:S(2)}, u32[]{:S(2)}) async-start(bf16[64,3,1,320,5]{3,1,4,2,0:T(4,128)(2,1)} %broadcast_in_dim.44), calls=%async_computation | async-start | bytes 1966080 | tf_op jit(solution)/shard_map/all_to_all | solution.py:21
  20.9 25.3 %all-to-all-done = bf16[64,3,1,320,5]{3,1,4,2,0:T(4,128)(2,1)S(1)} async-done(((bf16[64,3,1,320,5]{3,1,4,2,0:T(4,128)(2,1)}), bf16[64,3,1,320,5]{3,1,4,2,0:T(4,128)(2,1)S(1)}, u32[]{:S(2)}, u32[]{:S(2)}) %all-to-all-start) | async-done | bytes 614432 | tf_op jit(solution)/shard_map/all_to_all | solution.py:21
  46.2 3.9 %slice_reduce_fusion.3 = (bf16[320,64,5]{0,2,1:T(8,128)(2,1)S(1)}, bf16[320,64,5]{0,2,1:T(8,128)(2,1)S(1)}, bf16[320,64,5]{0,2,1:T(8,128)(2,1)S(1)}) fusion(bf16[3,1,320,64,5]{2,0,4,1,3:T(4,128)(2,1)S(1)} %bitcast.273), kind=kLoop, calls=%fused_computation.110 | loop fusion | bytes 1228800 | tf_op jit(solution)/shard_map/slice | solution.py:88
  51.2 4.1 %conditional.5 = (f32[1,1,320,64,5]{2,1,4,0,3:T(1,128)S(1)}, f32[1,1,320,64,5]{2,1,4,0,3:T(1,128)S(1)}, f32[1,1,320,64,5]{2,1,4,0,3:T(1,128)S(1)}) conditional(s32[]{:T(128)} %convert_element_type.69, () %tuple.51, (pred[256,1]{0,1:T(4,128)(4,1)S(1)}, f32[256,1]{0,1:T(1,128)S(1)}, bf16[256,1,320]{0,2,1:T(8,128)(2,1)S(1)}, ...), branch_computations={%region_4.5_spmd, %region_5.6_spmd} | conditional | flops 316867072 | bytes 11841872 | solution.py:112
  55.3 2.7 %maximum_bitcast_fusion = f32[64,3,1,320,5]{3,2,4,1,0:T(1,128)} fusion(f32[1,1,320,64,5]{2,1,4,0,3:T(1,128)S(1)} %get-tuple-element.272, f32[1,1,320,64,5]{2,1,4,0,3:T(1,128)S(1)} %get-tuple-element.271, f32[1,1,320,64,5]{2,1,4,0,3:T(1,128)S(1)} %get-tuple-element.270), kind=kLoop, calls=%fused_computation.94 | loop fusion | flops 614400 | bytes 2457600 | tf_op jit(solution)/shard_map/transpose | solution.py:39
  58.0 5.9 %all-to-all-start.1 = ((f32[64,3,1,320,5]{3,2,4,1,0:T(1,128)}), f32[64,3,1,320,5]{3,2,4,1,0:T(1,128)S(1)}, u32[]{:S(2)}, u32[]{:S(2)}) async-start(f32[64,3,1,320,5]{3,2,4,1,0:T(1,128)} %maximum_bitcast_fusion), calls=%async_computation.1 | async-start | bytes 2949120 | tf_op jit(solution)/shard_map/all_to_all | solution.py:44
  64.2 36.5 %all-to-all-done.1 = f32[64,3,1,320,5]{3,2,4,1,0:T(1,128)S(1)} async-done(((f32[64,3,1,320,5]{3,2,4,1,0:T(1,128)}), f32[64,3,1,320,5]{3,2,4,1,0:T(1,128)S(1)}, u32[]{:S(2)}, u32[]{:S(2)}) %all-to-all-start.1) | async-done | bytes 1228832 | tf_op jit(solution)/shard_map/all_to_all | solution.py:44
  100.6 1.1 reduce_sum.153
  102.2 1.2 broadcast_in_dim.46
  103.4 7.0 %all-to-all-start.2 = ((bf16[64,3,1,320,5]{3,1,4,2,0:T(4,128)(2,1)}), bf16[64,3,1,320,5]{3,1,4,2,0:T(4,128)(2,1)S(1)}, u32[]{:S(2)}, u32[]{:S(2)}) async-start(bf16[64,3,1,320,5]{3,1,4,2,0:T(4,128)(2,1)} %broadcast_in_dim.46), calls=%async_computation.2 | async-start | bytes 1966080 | tf_op jit(solution)/shard_map/all_to_all | solution.py:21
  111.1 0.8 conditional.4
  111.9 25.8 %all-to-all-done.2 = bf16[64,3,1,320,5]{3,1,4,2,0:T(4,128)(2,1)S(1)} async-done(((bf16[64,3,1,320,5]{3,1,4,2,0:T(4,128)(2,1)}), bf16[64,3,1,320,5]{3,1,4,2,0:T(4,128)(2,1)S(1)}, u32[]{:S(2)}, u32[]{:S(2)}) %all-to-all-start.2) | async-done | bytes 614432 | tf_op jit(solution)/shard_map/all_to_all | solution.py:21
  137.7 3.9 %slice_reduce_fusion = (bf16[320,64,5]{0,2,1:T(8,128)(2,1)S(1)}, bf16[320,64,5]{0,2,1:T(8,128)(2,1)S(1)}, bf16[320,64,5]{0,2,1:T(8,128)(2,1)S(1)}) fusion(bf16[3,1,320,64,5]{2,0,4,1,3:T(4,128)(2,1)S(1)} %bitcast.272), kind=kLoop, calls=%fused_computation.107 | loop fusion | bytes 1228800 | tf_op jit(solution)/shard_map/slice | solution.py:88
  143.3 6.6 %all-to-all-start.3 = ((f32[8,1,256]{2,1,0:T(1,128)}), f32[8,1,256]{2,1,0:T(1,128)S(1)}, u32[]{:S(2)}, u32[]{:S(2)}) async-start(f32[8,1,256]{2,1,0:T(1,128)} %broadcast_in_dim.47), calls=%async_computation.3 | async-start | bytes 16384 | tf_op jit(solution)/shard_map/all_to_all | solution.py:21
  149.9 1.0 conditional.7
  150.9 2.7 %maximum_bitcast_fusion.1 = f32[64,3,1,320,5]{3,2,4,1,0:T(1,128)} fusion(f32[1,1,320,64,5]{2,1,4,0,3:T(1,128)S(1)} %get-tuple-element.275, f32[1,1,320,64,5]{2,1,4,0,3:T(1,128)S(1)} %get-tuple-element.274, f32[1,1,320,64,5]{2,1,4,0,3:T(1,128)S(1)} %get-tuple-element.273), kind=kLoop, calls=%fused_computation.95 | loop fusion | flops 614400 | bytes 2457600 | tf_op jit(solution)/shard_map/transpose | solution.py:39
  153.6 5.2 %all-to-all-done.3 = f32[8,1,256]{2,1,0:T(1,128)S(1)} async-done(((f32[8,1,256]{2,1,0:T(1,128)}), f32[8,1,256]{2,1,0:T(1,128)S(1)}, u32[]{:S(2)}, u32[]{:S(2)}) %all-to-all-start.3) | async-done | bytes 8224 | tf_op jit(solution)/shard_map/all_to_all | solution.py:21
  158.8 8.1 %all-to-all-start.4 = ((f32[64,3,1,320,5]{3,2,4,1,0:T(1,128)}), f32[64,3,1,320,5]{3,2,4,1,0:T(1,128)S(1)}, u32[]{:S(2)}, u32[]{:S(2)}) async-start(f32[64,3,1,320,5]{3,2,4,1,0:T(1,128)} %maximum_bitcast_fusion.1), calls=%async_computation.4 | async-start | bytes 2949120 | tf_op jit(solution)/shard_map/all_to_all | solution.py:44
  166.9 3.3 %collective-permute-start.2 = (bf16[256,320]{0,1:T(8,128)(2,1)S(1)}, bf16[256,320]{0,1:T(8,128)(2,1)S(1)}, u32[]{:S(2)}, u32[]{:S(2)}) collective-permute-start(bf16[256,320]{0,1:T(8,128)(2,1)S(1)} %copy-done.1), channel_id=1, source_target_pairs={{0,16},{8,24},{16,32},{24,40},{32,48},{40,56},{48,64},{56,72},{64,... | collective-permute-start | bytes 491528 | tf_op jit(solution)/shard_map/ppermute | solution.py:16
  170.2 3.6 %collective-permute-start.3 = (bf16[256,320]{0,1:T(8,128)(2,1)S(1)}, bf16[256,320]{0,1:T(8,128)(2,1)S(1)}, u32[]{:S(2)}, u32[]{:S(2)}) collective-permute-start(bf16[256,320]{0,1:T(8,128)(2,1)S(1)} %copy-done.1), channel_id=1, source_target_pairs={{0,8},{8,16},{16,24},{24,32},{32,40},{40,48},{48,56},{56,64},{64,7... | collective-permute-start | bytes 491528 | tf_op jit(solution)/shard_map/ppermute | solution.py:16
  173.9 3.8 %collective-permute-start = (bf16[256,320]{0,1:T(8,128)(2,1)S(1)}, bf16[256,320]{0,1:T(8,128)(2,1)}, u32[]{:S(2)}, u32[]{:S(2)}) collective-permute-start(bf16[256,320]{0,1:T(8,128)(2,1)S(1)} %copy-done), channel_id=1, source_target_pairs={{0,16},{8,24},{16,32},{24,40},{32,48},{40,56},{48,64},{56,72},{64,... | collective-permute-start | bytes 491528 | tf_op jit(solution)/shard_map/ppermute | solution.py:16
  177.6 1.9 collective-permute-start.1
  179.6 14.5 %collective-permute-done.2 = bf16[256,320]{0,1:T(8,128)(2,1)S(1)} collective-permute-done((bf16[256,320]{0,1:T(8,128)(2,1)S(1)}, bf16[256,320]{0,1:T(8,128)(2,1)S(1)}, u32[]{:S(2)}, u32[]{:S(2)}) %collective-permute-start.2) | collective-permute-done | bytes 163872 | tf_op jit(solution)/shard_map/ppermute | solution.py:16
  194.1 3.5 %collective-permute-done.3 = bf16[256,320]{0,1:T(8,128)(2,1)S(1)} collective-permute-done((bf16[256,320]{0,1:T(8,128)(2,1)S(1)}, bf16[256,320]{0,1:T(8,128)(2,1)S(1)}, u32[]{:S(2)}, u32[]{:S(2)}) %collective-permute-start.3) | collective-permute-done | bytes 163872 | tf_op jit(solution)/shard_map/ppermute | solution.py:16
  198.2 1.5 fusion.107
  200.2 1.4 collective-permute-done.1
  201.6 2.3 %fusion.80 = bf16[256,320]{0,1:T(8,128)(2,1)} fusion(bf16[256,320]{0,1:T(8,128)(2,1)S(1)} %copy-done, bf16[256,320]{0,1:T(8,128)(2,1)} %collective-permute-done.1, bf16[256,320]{0,1:T(8,128)(2,1)} %collective-permute-done, f32[256,768]{0,1:T(8,128)S(1)} %get-tuple-element.307, f32[256]{0:T(256)S(1)} %fusion.81, f32[256]{0:T(256)S(1)} %get-tuple-element.306, ...), kind=kOutput, calls=%fused_computation.102 | convolution fusion | flops 129286144 | bytes 2107648 | tf_op jit(solution)/shard_map/hqk,khd->qhd/dot_general | solution.py:159
  203.9 10.8 %all-to-all-done.4 = f32[64,3,1,320,5]{3,2,4,1,0:T(1,128)S(1)} async-done(((f32[64,3,1,320,5]{3,2,4,1,0:T(1,128)}), f32[64,3,1,320,5]{3,2,4,1,0:T(1,128)S(1)}, u32[]{:S(2)}, u32[]{:S(2)}) %all-to-all-start.4) | async-done | bytes 1228832 | tf_op jit(solution)/shard_map/all_to_all | solution.py:44
  214.7 1.1 reduce_sum.163
  (88 shorter events, 12.9 us)
Async XLA Ops:
  3.5 42.7 %all-to-all-start = ((bf16[64,3,1,320,5]{3,1,4,2,0:T(4,128)(2,1)}), bf16[64,3,1,320,5]{3,1,4,2,0:T(4,128)(2,1)S(1)}, u32[]{:S(2)}, u32[]{:S(2)}) async-start(bf16[64,3,1,320,5]{3,1,4,2,0:T(4,128)(2,1)} %broadcast_in_dim.44), calls=%async_computation | async-start | bytes 1966080 | tf_op jit(solution)/shard_map/all_to_all | solution.py:21
  50.2 0.9 copy-start
  50.2 1.0 copy-start.1
  50.2 1.0 copy-start.12
  52.0 0.7 copy-start.5
  53.6 1.0 copy-start.6
  58.0 5.9 %copy-start.9 = (f32[1,320,5]{1,0,2:T(1,128)S(1)}, f32[1,320,5]{1,0,2:T(1,128)}, u32[]{:S(2)}) copy-start(f32[1,320,5]{1,0,2:T(1,128)} %param.24) | copy-start | bytes 19204
  58.0 6.0 %copy-start.10 = (f32[1,320,5]{1,0,2:T(1,128)S(1)}, f32[1,320,5]{1,0,2:T(1,128)}, u32[]{:S(2)}) copy-start(f32[1,320,5]{1,0,2:T(1,128)} %param.25) | copy-start | bytes 19204
  58.0 42.6 %all-to-all-start.1 = ((f32[64,3,1,320,5]{3,2,4,1,0:T(1,128)}), f32[64,3,1,320,5]{3,2,4,1,0:T(1,128)S(1)}, u32[]{:S(2)}, u32[]{:S(2)}) async-start(f32[64,3,1,320,5]{3,2,4,1,0:T(1,128)} %maximum_bitcast_fusion), calls=%async_computation.1 | async-start | bytes 2949120 | tf_op jit(solution)/shard_map/all_to_all | solution.py:44
  63.9 37.9 %copy-start.11 = (f32[1,320,5]{1,0,2:T(1,128)S(1)}, f32[1,320,5]{1,0,2:T(1,128)}, u32[]{:S(2)}) copy-start(f32[1,320,5]{1,0,2:T(1,128)} %param.26) | copy-start | bytes 19204
  102.2 8.8 %copy-start.2 = (bf16[256,320]{0,1:T(8,128)(2,1)S(1)}, bf16[256,320]{0,1:T(8,128)(2,1)}, u32[]{:S(2)}) copy-start(bf16[256,320]{0,1:T(8,128)(2,1)} %param.18) | copy-start | bytes 491524
  103.4 34.3 %all-to-all-start.2 = ((bf16[64,3,1,320,5]{3,1,4,2,0:T(4,128)(2,1)}), bf16[64,3,1,320,5]{3,1,4,2,0:T(4,128)(2,1)S(1)}, u32[]{:S(2)}, u32[]{:S(2)}) async-start(bf16[64,3,1,320,5]{3,1,4,2,0:T(4,128)(2,1)} %broadcast_in_dim.46), calls=%async_computation.2 | async-start | bytes 1966080 | tf_op jit(solution)/shard_map/all_to_all | solution.py:21
  141.7 0.9 copy-start.3
  143.3 15.5 %all-to-all-start.3 = ((f32[8,1,256]{2,1,0:T(1,128)}), f32[8,1,256]{2,1,0:T(1,128)S(1)}, u32[]{:S(2)}, u32[]{:S(2)}) async-start(f32[8,1,256]{2,1,0:T(1,128)} %broadcast_in_dim.47), calls=%async_computation.3 | async-start | bytes 16384 | tf_op jit(solution)/shard_map/all_to_all | solution.py:21
  153.6 25.9 %copy-start.13 = (s32[256]{0:T(256)S(1)}, s32[256]{0:T(256)}, u32[]{:S(2)}) copy-start(s32[256]{0:T(256)} %param.22) | copy-start | bytes 3076
  153.6 44.6 %copy-start.4 = (bf16[256,320]{0,1:T(8,128)(2,1)S(1)}, bf16[256,320]{0,1:T(8,128)(2,1)}, u32[]{:S(2)}) copy-start(bf16[256,320]{0,1:T(8,128)(2,1)} %param.18) | copy-start | bytes 491524
  158.8 55.8 %all-to-all-start.4 = ((f32[64,3,1,320,5]{3,2,4,1,0:T(1,128)}), f32[64,3,1,320,5]{3,2,4,1,0:T(1,128)S(1)}, u32[]{:S(2)}, u32[]{:S(2)}) async-start(f32[64,3,1,320,5]{3,2,4,1,0:T(1,128)} %maximum_bitcast_fusion.1), calls=%async_computation.4 | async-start | bytes 2949120 | tf_op jit(solution)/shard_map/all_to_all | solution.py:44
  166.9 27.1 %collective-permute-start.2 = (bf16[256,320]{0,1:T(8,128)(2,1)S(1)}, bf16[256,320]{0,1:T(8,128)(2,1)S(1)}, u32[]{:S(2)}, u32[]{:S(2)}) collective-permute-start(bf16[256,320]{0,1:T(8,128)(2,1)S(1)} %copy-done.1), channel_id=1, source_target_pairs={{0,16},{8,24},{16,32},{24,40},{32,48},{40,56},{48,64},{56,72},{64,... | collective-permute-start | bytes 491528 | tf_op jit(solution)/shard_map/ppermute | solution.py:16
  170.2 27.4 %collective-permute-start.3 = (bf16[256,320]{0,1:T(8,128)(2,1)S(1)}, bf16[256,320]{0,1:T(8,128)(2,1)S(1)}, u32[]{:S(2)}, u32[]{:S(2)}) collective-permute-start(bf16[256,320]{0,1:T(8,128)(2,1)S(1)} %copy-done.1), channel_id=1, source_target_pairs={{0,8},{8,16},{16,24},{24,32},{32,40},{40,48},{48,56},{56,64},{64,7... | collective-permute-start | bytes 491528 | tf_op jit(solution)/shard_map/ppermute | solution.py:16
  173.9 26.3 %collective-permute-start = (bf16[256,320]{0,1:T(8,128)(2,1)S(1)}, bf16[256,320]{0,1:T(8,128)(2,1)}, u32[]{:S(2)}, u32[]{:S(2)}) collective-permute-start(bf16[256,320]{0,1:T(8,128)(2,1)S(1)} %copy-done), channel_id=1, source_target_pairs={{0,16},{8,24},{16,32},{24,40},{32,48},{40,56},{48,64},{56,72},{64,... | collective-permute-start | bytes 491528 | tf_op jit(solution)/shard_map/ppermute | solution.py:16
  177.6 24.0 %collective-permute-start.1 = (bf16[256,320]{0,1:T(8,128)(2,1)S(1)}, bf16[256,320]{0,1:T(8,128)(2,1)}, u32[]{:S(2)}, u32[]{:S(2)}) collective-permute-start(bf16[256,320]{0,1:T(8,128)(2,1)S(1)} %copy-done), channel_id=1, source_target_pairs={{0,8},{8,16},{16,24},{24,32},{32,40},{40,48},{48,56},{56,64},{64,7... | collective-permute-start | bytes 491528 | tf_op jit(solution)/shard_map/ppermute | solution.py:16
  194.1 3.5 %copy-start.14 = (bf16[256,320]{0,1:T(8,128)(2,1)}, bf16[256,320]{0,1:T(8,128)(2,1)S(1)}, u32[]{:S(2)}) copy-start(bf16[256,320]{0,1:T(8,128)(2,1)S(1)} %collective-permute-done.2) | copy-start | bytes 491524
  197.6 0.7 copy-start.15
  198.2 3.4 %copy-start.16 = (f32[320]{0:T(512)S(1)}, f32[320]{0:T(512)}, u32[]{:S(2)}) copy-start(f32[320]{0:T(512)} %param.27) | copy-start | bytes 3844
where the time goes:
time: 220 us; the launch traced here: 218 us
  waiting for transfers between devices  123 us (56%)
  starting transfers between devices  55.5 us (25%)
  local copies, waits for them, and re-layouts  19.2 us (9%)
  other arithmetic  10.8 us (5%)
  matrix products  6.26 us (3%)
  between operations  2.91 us (1%)
    all_to_all x3, waiting for transfers between devices, from_everyone(): lax.all_to_all(jnp.broadcast_to(array[None], (peers, *array.shape)), axis...  56.4 us
    all_to_all x2, waiting for transfers between devices, sum_at_owner(): lax.all_to_all(parts, axis, split_axis=0, concat_axis=0, tiled=True)  47.3 us
    all_to_all x3, starting transfers between devices, from_everyone(): lax.all_to_all(jnp.broadcast_to(array[None], (peers, *array.shape)), axis...  28.9 us
    ppermute x4, waiting for transfers between devices, shifted(): lax.ppermute(value, axis, [(source, source + steps) for source in range(f...  19.4 us
    all_to_all x2, starting transfers between devices, sum_at_owner(): lax.all_to_all(parts, axis, split_axis=0, concat_axis=0, tiled=True)  14 us
    ppermute x4, starting transfers between devices, shifted(): lax.ppermute(value, axis, [(source, source + steps) for source in range(f...  12.6 us
    slice x2, local copies, waits for them, and re-layouts, unstack(): return (stacked[0], stacked[1], stacked[2])  7.89 us
    transpose x2, other arithmetic, split_up(): return jnp.moveaxis(array.reshape(*before, peers, -1, *after), dim, 0)  5.43 us
  transfers between devices with their start and end apart: 9, of which 8 were waited for; matrix products, arithmetic and copies ran while one was open for 4% of the time, Pallas kernels for 0%

commit v1 on v0

v1 whole, which is shorter than its diff:
```python
import functools
import math

import jax
import jax.numpy as jnp
import numpy as np
from jax import lax
from jax.experimental import pallas as pl
from jax.experimental.pallas import tpu as pltpu
from jax.sharding import PartitionSpec as P

HEADS = 8
HD = 320
FH = 320
WINDOW = 512
NZ, NY, NC = 8, 4, 2
CHIPS = NZ * NY
OWN = 5
SLOT = 16
ZROWS = NY * NC * OWN
FAR_FIRST = (4, 3, 5, 2, 6, 1, 7, 0)
NEAR_FIRST = (0, 1, 7, 2, 6, 3, 5, 4)
F32, BF16 = jnp.float32, jnp.bfloat16


def nn(a, b):
    return lax.dot_general(a, b, (((1,), (0,)), ((), ())), preferred_element_type=F32)


def nt(a, b):
    return lax.dot_general(a, b, (((1,), (1,)), ((), ())), preferred_element_type=F32)


def tn(a, b):
    return lax.dot_general(a, b, (((0,), (0,)), ((), ())), preferred_element_type=F32)


def order_matrix():
    perm = np.zeros((128, 128), np.float32)
    for m in range(3):
        for y in range(NY):
            for c in range(NC):
                for j in range(OWN):
                    perm[m * ZROWS + (y * NC + c) * OWN + j, c * 64 + y * SLOT + m * OWN + j] = 1.0
    return perm


def kernel(
    ge, q, k, v, rates, back, s0, gain, perm, perm_t,
    out, s2,
    own, ag, gs, cr, red, rr, kv_far, kv_near, sq, sqr, nat, gt, ut, dt, es, y_buf, at_buf, state,
    ag_send, ag_recv, fw_send, fw_recv, cs_send, cs_recv, rs_send, rs_recv, kv_send, kv_recv, sq_send, sq_recv,
):
    rows = q.shape[0]
    t = lax.axis_index("tok")
    h = lax.axis_index("head")
    c = lax.rem(t, 2)
    chip = lax.div(t, 2)
    zme = lax.div(chip, NY)
    yme = lax.rem(chip, NY)
    mate = t + 1 - 2 * c

    def at_chip(p):
        return {"tok": 2 * p + c}

    barrier = pltpu.get_barrier_semaphore()

    def greet(i, _):
        pl.semaphore_signal(barrier, inc=1, device_id=at_chip(lax.rem(chip + i, CHIPS)))
        return 0

    lax.fori_loop(1, CHIPS, greet, 0)
    pl.semaphore_signal(barrier, inc=1, device_id={"tok": mate})

    def greet_head(i, _):
        pl.semaphore_signal(barrier, inc=1, device_id={"head": lax.rem(h + i, HEADS)})
        return 0

    lax.fori_loop(1, HEADS, greet_head, 0)

    start = t * rows
    pos = start + lax.broadcasted_iota(jnp.int32, (rows, 1), 0)
    first = pos < ge[0]
    rate = rates[...]
    vf = v[...].astype(F32)
    es[0] = (-jnp.where(first, rate, 0.0) * vf).astype(BF16)
    es[1] = (-jnp.where(first, 0.0, rate) * vf).astype(BF16)
    state[...] = s0[...]
    own[0] = s0[...].astype(BF16)

    pl.semaphore_wait(barrier, (CHIPS - 1) + 1 + (HEADS - 1))

    def peers(dzs, body):
        for dz in dzs:
            zz = lax.rem(zme + dz, NZ)
            for dy in range(NY):
                yy = lax.rem(yme + dy, NY)
                body(zz, yy, dz == 0 and dy == 0)

    def gather_start(g):
        mine = ag.at[g, c, chip]

        def send(zz, yy, is_me):
            if is_me:
                pltpu.make_async_copy(own.at[g], mine, ag_recv.at[g, zme]).start()
            else:
                pltpu.make_async_remote_copy(
                    own.at[g], mine, ag_send.at[g], ag_recv.at[g, zme], at_chip(zz * NY + yy)
                ).start()

        peers(FAR_FIRST, send)

    def gather_forward(g):
        for dz in NEAR_FIRST:
            zz = lax.rem(zme + dz, NZ)
            four = ag.at[g, c, pl.ds(zz * NY, NY)]
            pltpu.make_async_copy(four, four, ag_recv.at[g, zz]).wait()
            pltpu.make_async_remote_copy(four, four, fw_send.at[g], fw_recv.at[g, zz], {"tok": mate}).start()

    def gather_finish(g):
        for z in range(NZ):
            four = ag.at[g, 1 - c, pl.ds(z * NY, NY)]
            pltpu.make_async_copy(four, four, fw_recv.at[g, z]).wait()
            block = ag[g, :, z * NY : (z + 1) * NY].reshape(NC * NY * SLOT, HD)
            ordered = nn(perm[...], block)
            for m in range(3):
                nat[m, z * ZROWS : (z + 1) * ZROWS] = ordered[m * ZROWS : (m + 1) * ZROWS]
        gt[...] = nat[0].astype(BF16)
        ut[...] = nat[1].astype(BF16)
        dt[...] = nat[2].astype(BF16)

    def gather_drain(g):
        thirty_one = ag.at[g, 0, pl.ds(0, CHIPS - 1)]
        pltpu.make_async_copy(thirty_one, thirty_one, ag_send.at[g]).wait()
        every = ag.at[g, 0]
        pltpu.make_async_copy(every, every, fw_send.at[g]).wait()

    def grads(g):
        kk, e = k[...], es[g]
        a = nt(kk, gt[...])
        b = nt(kk, ut[...])
        s = jax.nn.sigmoid(a)
        active = a * s
        r = (active * b).astype(BF16)
        du = nn(e, dt[...])
        da = (du * b * s * (1.0 + a * (1.0 - s))).astype(BF16)
        db = (du * active).astype(BF16)
        nat[0] = tn(da, kk)
        nat[1] = tn(db, kk)
        nat[2] = tn(e, r)

    def reduce_start(g):
        for z in range(NZ):
            part = [nat[m, z * ZROWS : (z + 1) * ZROWS] for m in range(3)]
            part.append(jnp.zeros((128 - 3 * ZROWS, HD), F32))
            block = nn(perm_t[...], jnp.concatenate(part, axis=0).astype(BF16)).astype(BF16)
            gs[g, :, z * NY : (z + 1) * NY] = block.reshape(NC, NY, SLOT, HD)
            pltpu.make_async_remote_copy(
                gs.at[g, 1 - c, pl.ds(z * NY, NY)], cr.at[g, pl.ds(z * NY, NY)],
                cs_send.at[g], cs_recv.at[g, z], {"tok": mate},
            ).start()
        for dz in FAR_FIRST:
            zz = lax.rem(zme + dz, NZ)
            here = pl.ds(zz * NY, NY)
            four = cr.at[g, here]
            pltpu.make_async_copy(four, four, cs_recv.at[g, zz]).wait()
            red[g, here] = (gs[g, c, here].astype(F32) + cr[g, here].astype(F32)).astype(BF16)

            def send(z_to, yy, is_me):
                p = z_to * NY + yy
                if is_me:
                    pltpu.make_async_copy(red.at[g, p], rr.at[g, chip], rs_recv.at[g]).start()
                else:
                    pltpu.make_async_remote_copy(
                        red.at[g, p], rr.at[g, chip], rs_send.at[g], rs_recv.at[g], at_chip(p)
                    ).start()

            peers((dz,), send)

    def reduce_finish(g):
        every = rr.at[g]
        pltpu.make_async_copy(every, every, rs_recv.at[g]).wait()
        total = jnp.sum(rr[g].astype(F32), axis=0)
        old = state[...]
        fresh = old - total
        old_norm = jnp.sqrt(jnp.sum(old * old, axis=1, keepdims=True))
        new_norm = jnp.sqrt(jnp.sum(fresh * fresh, axis=1, keepdims=True) + 1e-06)
        return fresh * (old_norm / new_norm)

    def reduce_drain(g):
        every = cr.at[g]
        pltpu.make_async_copy(every, every, cs_send.at[g]).wait()
        thirty_one = rr.at[g, pl.ds(0, CHIPS - 1)]
        pltpu.make_async_copy(thirty_one, thirty_one, rs_send.at[g]).wait()

    def apply_queries():
        a = nt(q[...], gt[...])
        b = nt(q[...], ut[...])
        hidden = (a * jax.nn.sigmoid(a) * b).astype(BF16)
        return nt(hidden, dt[...])

    gather_start(0)

    nxt = at_chip(lax.rem(chip + 1, CHIPS))
    far_copies = [
        pltpu.make_async_remote_copy(src, kv_far.at[i], kv_send.at[i], kv_recv.at[i], nxt) for i, src in enumerate((k, v))
    ]
    for copy in far_copies:
        copy.start()

    def near_copies(srcs):
        return [
            pltpu.make_async_remote_copy(src, kv_near.at[i], kv_send.at[2 + i], kv_recv.at[2 + i], {"tok": mate})
            for i, src in enumerate(srcs)
        ]

    @pl.when(c == 0)
    def _():
        for copy in near_copies((k, v)):
            copy.start()

    gather_forward(0)
    gather_finish(0)
    grads(0)
    reduce_start(0)
    y_buf[...] = apply_queries()
    for copy in far_copies:
        copy.wait()

    @pl.when(c == 1)
    def _():
        for copy in near_copies((kv_far.at[0], kv_far.at[1])):
            copy.start()

    middle = reduce_finish(0)
    state[...] = middle
    own[1] = middle.astype(BF16)
    gather_start(1)

    for copy in near_copies((kv_far.at[0], kv_far.at[1])):
        copy.wait()
    qq = q[...]
    scale = 1.0 / math.sqrt(HD)
    i = lax.broadcasted_iota(jnp.int32, (rows, rows), 0)
    j = lax.broadcasted_iota(jnp.int32, (rows, rows), 1)
    reach = back[...]
    scores = []
    for ahead, keys in ((2 * rows, kv_far.at[0]), (rows, kv_near.at[0]), (0, k)):
        away = i - j + ahead
        seen = (away >= 0) & (away <= reach) & (start + j - ahead >= 0)
        scores.append((jnp.where(seen, nt(qq, keys[...]) * scale, -jnp.inf)))
    top = functools.reduce(jnp.maximum, [jnp.max(s, axis=1, keepdims=True) for s in scores])
    weights = [jnp.exp(s - top) for s in scores]
    total = functools.reduce(jnp.add, [jnp.sum(w, axis=1, keepdims=True) for w in weights])
    pieces = [
        nn((w / total).astype(BF16), vals[...]) for w, vals in zip(weights, (kv_far.at[1], kv_near.at[1], v))
    ]
    at_buf[...] = pieces[0] + pieces[1] + pieces[2]

    gather_forward(1)
    gather_finish(1)
    grads(1)
    reduce_start(1)
    mixed = jnp.where(first, y_buf[...], apply_queries())
    y_buf[...] = mixed
    sums = lax.dot_general(
        jnp.ones((8, HD), F32), mixed * mixed, (((1,), (1,)), ((), ())),
        precision=lax.Precision.HIGHEST, preferred_element_type=F32,
    )
    sq[...] = sums
    sqr[h] = sums

    def send_squares(n, _):
        pltpu.make_async_remote_copy(sq, sqr.at[h], sq_send, sq_recv, {"head": lax.rem(h + n, HEADS)}).start()
        return 0

    lax.fori_loop(1, HEADS, send_squares, 0)
    seven = sqr.at[pl.ds(0, HEADS - 1)]
    pltpu.make_async_copy(seven, seven, sq_recv).wait()
    squares = jnp.sum(sqr[...], axis=0).T[:, 0:1]
    mean_square = squares / (HEADS * HD)
    normed = y_buf[...] / jnp.sqrt(mean_square + 1e-06) * gain[...]
    out[...] = (normed + at_buf[...]).astype(BF16)
    s2[...] = reduce_finish(1)
    pltpu.make_async_copy(seven, seven, sq_send).wait()
    for g in range(2):
        gather_drain(g)
        reduce_drain(g)


def on_device(queries, keys, values, rates, back, group_end, gate_init, up_init, down_init, gain):
    rows = rates.shape[0]
    perm = order_matrix()
    shares = (gate_init[0].T, up_init[0].T, down_init[0].T)
    s0 = jnp.concatenate((*shares, jnp.zeros((SLOT - 3 * OWN, HD), F32)), axis=0)
    vmem = pl.BlockSpec(memory_space=pltpu.VMEM)
    slots = (CHIPS, SLOT, HD)
    dma = pltpu.SemaphoreType.DMA
    out, s2 = pl.pallas_call(
        kernel,
        out_shape=(
            jax.ShapeDtypeStruct((rows, HD), BF16),
            jax.ShapeDtypeStruct((SLOT, HD), F32),
        ),
        in_specs=[pl.BlockSpec(memory_space=pltpu.SMEM)] + [vmem] * 9,
        out_specs=(vmem, vmem),
        scratch_shapes=[
            pltpu.VMEM((2, SLOT, HD), BF16),
            pltpu.VMEM((2, NC, *slots), BF16),
            pltpu.VMEM((2, NC, *slots), BF16),
            pltpu.VMEM((2, *slots), BF16),
            pltpu.VMEM((2, *slots), BF16),
            pltpu.VMEM((2, *slots), BF16),
            pltpu.VMEM((2, rows, HD), BF16),
            pltpu.VMEM((2, rows, HD), BF16),
            pltpu.VMEM((8, rows), F32),
            pltpu.VMEM((HEADS, 8, rows), F32),
            pltpu.VMEM((3, HD, HD), F32),
            pltpu.VMEM((FH, HD), BF16),
            pltpu.VMEM((FH, HD), BF16),
            pltpu.VMEM((HD, FH), BF16),
            pltpu.VMEM((2, rows, HD), BF16),
            pltpu.VMEM((rows, HD), F32),
            pltpu.VMEM((rows, HD), F32),
            pltpu.VMEM((SLOT, HD), F32),
            dma((2,)), dma((2, NZ)),
            dma((2,)), dma((2, NZ)),
            dma((2,)), dma((2, NZ)),
            dma((2,)), dma((2,)),
            dma((4,)), dma((4,)),
            dma, dma,
        ],
        compiler_params=pltpu.CompilerParams(
            collective_id=0, has_side_effects=True, vmem_limit_bytes=48 * 1024 * 1024
        ),
        name="layer",
    )(
        group_end, queries, keys, values, rates, back.reshape(rows, 1), s0, gain.reshape(1, HD),
        jnp.asarray(perm, BF16), jnp.asarray(perm.T, BF16),
    )
    finals = [s2[m * OWN : (m + 1) * OWN].T[None] for m in range(3)]
    return (out, *finals)


def solution(mesh):
    placed = (
        P("tok", "head"),
        P("tok", "head"),
        P("tok", "head"),
        P("tok", "head"),
        P("tok"),
        P(),
        P("head", None, "tok"),
        P("head", None, "tok"),
        P("head", None, "tok"),
        P("head"),
    )
    return jax.shard_map(
        on_device,
        mesh=mesh,
        in_specs=placed,
        out_specs=(
            P("tok", "head"),
            P("head", None, "tok"),
            P("head", None, "tok"),
            P("head", None, "tok"),
        ),
        check_vma=False,
    )
```

time: 220 us -> 92.8 us (0.42)
  waiting for transfers between devices: 123 us -> 0 us
  Pallas kernels: 0 us -> 82.7 us
  starting transfers between devices: 55.5 us -> 0 us
  local copies, waits for them, and re-layouts: 19.2 us -> 8.07 us
  other arithmetic: 10.8 us -> 0.07 us
  matrix products: 6.26 us -> 0 us
    all_to_all x5 -> x0, waiting for transfers between devices: 104 us -> none  [the longest x3 56.4 us: from_everyone(): lax.all_to_all(jnp.broadcast_to(array[None], (peers, *array.shape)), axis...]
    pallas_call x0 -> x1, Pallas kernels: none -> 82.7 us  [on_device(): pl.pallas_call(kernel, out_shape=(jax.ShapeDtypeStruct((rows, HD), BF16),...]
    all_to_all x5 -> x0, starting transfers between devices: 42.9 us -> none  [the longest x3 28.9 us: from_everyone(): lax.all_to_all(jnp.broadcast_to(array[None], (peers, *array.shape)), axis...]
    ppermute x4 -> x0, waiting for transfers between devices: 19.4 us -> none  [shifted(): lax.ppermute(value, axis, [(source, source + steps) for source in range(f...]
    ppermute x4 -> x0, starting transfers between devices: 12.6 us -> none  [shifted(): lax.ppermute(value, axis, [(source, source + steps) for source in range(f...]
    slice x2 -> x0, local copies, waits for them, and re-layouts: 7.89 us -> none  [unstack(): return (stacked[0], stacked[1], stacked[2])]
    dot_general x10 -> x0, matrix products: 6.26 us -> none  [the longest x1 2.26 us: on_device(): jnp.einsum('hqk,khd->qhd', probs, value_ext, preferred_element_type=jnp.f...]
    transpose x2 -> x0, other arithmetic: 5.43 us -> none  [split_up(): return jnp.moveaxis(array.reshape(*before, peers, -1, *after), dim, 0)]
  transfers between devices with their start and end apart: 9 -> 0, of which waited for: 8 -> 0; matrix products, arithmetic and copies ran while one was open for 4% -> 0% of each run, Pallas kernels for 0% -> 0%
where the time goes in v1:
time: 92.8 us; the launch traced here: 92.2 us
  Pallas kernels  82.7 us (89%)
  local copies, waits for them, and re-layouts  8.07 us (9%)
  between operations  1.37 us (1%)
    pallas_call x1, Pallas kernels, on_device(): pl.pallas_call(kernel, out_shape=(jax.ShapeDtypeStruct((rows, HD), BF16),...  82.7 us
    unnamed x29, local copies, waits for them, and re-layouts  7.18 us

profile of v1, /device:TPU:1, one launch (start us, length us, event | category | flops | bytes accessed | tf_op | source)
XLA Modules:
  0.0 92.2 jit_solution(17311805750931330245)
XLA Ops:
  0.6 0.0 copy-start.7
  1.3 0.1 pad.3.clone
  1.4 0.7 reshape.15.gain
  2.1 0.0 copy-done.7
  2.1 0.0 copy-start.5
  2.1 0.0 copy-start.6
  2.1 0.7 copy-done.5
  2.8 0.0 copy-done.6
  2.8 0.0 copy-start.8
  2.8 0.0 copy-start.2
  2.8 0.1 maximum_maximum_fusion.s0
  2.9 0.6 copy-done.8
  3.5 0.0 copy-start.9
  3.5 0.1 copy.27.rates
  3.6 0.5 copy-done.9
  4.1 0.1 copy.28.back
  4.3 0.0 copy-done.2
  4.3 0.0 copy-start.3
  4.3 0.2 copy.24.q
  4.5 0.7 copy-done.3
  5.2 0.0 copy-start.4
  5.2 0.2 copy.25.k
  5.4 0.7 copy-done.4
  6.1 0.0 copy-start
  6.1 0.2 copy.26.v
  6.3 0.6 copy-done
  6.9 0.0 copy-done.1
  6.9 82.7 %layer.1 = (bf16[256,320]{1,0:T(8,128)(2,1)S(1)}, f32[16,320]{1,0:T(8,128)S(1)}) custom-call(s32[1]{0:T(128)S(6)} %copy.40.ge, bf16[256,320]{1,0:T(8,128)(2,1)S(1)} %copy.24.q, bf16[256,320]{1,0:T(8,128)(2,1)S(1)} %copy.25.k, bf16[256,320]{1,0:T(8,128)(2,1)S(1)} %copy.26.v, f32[256,1]{1,0:T(8,128)S(1)} %copy.27.rates, s32[256,1]{1,0:T(8,128)S(1)} %copy.28.back, ...), custom_call_target="tpu_custom_call" | custom-call | tf_op jit(solution)/shard_map/layer/pallas_call | solution.py:299
  89.6 0.8 copy.29
  90.4 0.6 copy.32
  91.0 0.6 copy.31
  91.6 0.6 copy.30
  (4 shorter events, 0.0 us)
Async XLA Ops:
  0.6 1.4 %copy-start.7 = (f32[1,320,5]{1,0,2:T(1,128)S(1)}, f32[1,320,5]{1,0,2:T(1,128)}, u32[]{:S(2)}) copy-start(f32[1,320,5]{1,0,2:T(1,128)} %param.18) | copy-start | bytes 19204
  2.1 0.7 copy-start.5
  2.1 0.7 copy-start.6
  2.8 0.7 copy-start.8
  2.8 1.5 %copy-start.2 = (bf16[256,320]{0,1:T(8,128)(2,1)S(1)}, bf16[256,320]{0,1:T(8,128)(2,1)}, u32[]{:S(2)}) copy-start(bf16[256,320]{0,1:T(8,128)(2,1)} %param.12) | copy-start | bytes 491524
  3.5 0.7 copy-start.9
  4.3 0.9 copy-start.3
  5.2 0.9 copy-start.4
  6.1 0.8 copy-start
  6.1 0.8 copy-start.1

commit v2 on v1

v2 whole, which is shorter than its diff:
```python
import functools
import math

import jax
import jax.numpy as jnp
import numpy as np
from jax import lax
from jax.experimental import pallas as pl
from jax.experimental.pallas import tpu as pltpu
from jax.sharding import PartitionSpec as P

HEADS = 8
HD = 320
FH = 320
WINDOW = 512
NZ, NY, NC = 8, 4, 2
CHIPS = NZ * NY
OWN = 5
SLOT = 16
ZROWS = NY * NC * OWN
LAST_FIRST = 12288 * NZ // 16384
FIRST_SECOND = 4096 * NZ // 16384
FAR_FIRST = (4, 3, 5, 2, 6, 1, 7, 0)
NEAR_FIRST = (0, 1, 7, 2, 6, 3, 5, 4)
F32, BF16 = jnp.float32, jnp.bfloat16


def nn(a, b):
    return lax.dot_general(a, b, (((1,), (0,)), ((), ())), preferred_element_type=F32)


def nt(a, b):
    return lax.dot_general(a, b, (((1,), (1,)), ((), ())), preferred_element_type=F32)


def tn(a, b):
    return lax.dot_general(a, b, (((0,), (0,)), ((), ())), preferred_element_type=F32)


def order_matrix():
    perm = np.zeros((128, 128), np.float32)
    for m in range(3):
        for y in range(NY):
            for c in range(NC):
                for j in range(OWN):
                    perm[m * ZROWS + (y * NC + c) * OWN + j, c * 64 + y * SLOT + m * OWN + j] = 1.0
    return perm


def kernel(
    ge, q_hbm, k_hbm, v_hbm, rates_hbm, back_hbm, g_hbm, u_hbm, d_hbm, gain_hbm, perm, perm_t,
    out, g_out, u_out, d_out,
    q, k, v, rates, back, rows0, gain,
    own, ag, gs, cr, red, rr, kv_far, kv_near, sq, sqr, nat, gt, ut, dt, es, y_buf, probs, state,
    in_sem, ag_send, ag_recv, fw_send, fw_recv, cs_send, cs_recv, rs_send, rs_recv, kv_send, kv_recv, sq_send, sq_recv,
):
    toks = q.shape[1]
    t = lax.axis_index("tok")
    h = lax.axis_index("head")
    c = lax.rem(t, 2)
    chip = lax.div(t, 2)
    zme = lax.div(chip, NY)
    yme = lax.rem(chip, NY)
    mate = t + 1 - 2 * c

    loads = [
        pltpu.make_async_copy(src, dst, in_sem.at[n])
        for n, (src, dst) in enumerate(
            (
                (g_hbm, rows0.at[pl.ds(0, OWN)]),
                (u_hbm, rows0.at[pl.ds(OWN, OWN)]),
                (d_hbm, rows0.at[pl.ds(2 * OWN, OWN)]),
                (k_hbm, k),
                (v_hbm, v),
                (q_hbm, q),
                (rates_hbm, rates),
                (back_hbm, back),
                (gain_hbm, gain),
            )
        )
    ]
    for load in loads:
        load.start()

    def at_chip(p):
        return {"tok": 2 * p + c}

    barrier = pltpu.get_barrier_semaphore()

    def greet(i, _):
        pl.semaphore_signal(barrier, inc=1, device_id=at_chip(lax.rem(chip + i, CHIPS)))
        return 0

    lax.fori_loop(1, CHIPS, greet, 0)
    pl.semaphore_signal(barrier, inc=1, device_id={"tok": mate})

    def greet_head(i, _):
        pl.semaphore_signal(barrier, inc=1, device_id={"head": lax.rem(h + i, HEADS)})
        return 0

    lax.fori_loop(1, HEADS, greet_head, 0)

    rows0[pl.ds(3 * OWN, 1)] = jnp.zeros((1, 1, HD), F32)
    for load in loads:
        load.wait()
    state[...] = rows0[...].reshape(SLOT, HD)
    own[0] = state[...].astype(BF16)
    start = t * toks
    first = start + lax.broadcasted_iota(jnp.int32, (1, toks), 1) < ge[0]
    rate = rates[...]
    vf = v[...].astype(F32)
    es[0] = (-jnp.where(first, rate, 0.0) * vf).astype(BF16)
    es[1] = (-jnp.where(first, 0.0, rate) * vf).astype(BF16)
    y_buf[...] = jnp.zeros_like(y_buf)

    pl.semaphore_wait(barrier, (CHIPS - 1) + 1 + (HEADS - 1))

    def active(g, z):
        return z < LAST_FIRST if g == 0 else z >= FIRST_SECOND

    live = [active(g, zme) for g in range(2)]
    z_from = (0, FIRST_SECOND)

    def peers(dzs, body):
        for dz in dzs:
            zz = lax.rem(zme + dz, NZ)
            for dy in range(NY):
                yy = lax.rem(yme + dy, NY)
                body(zz, yy, dz == 0 and dy == 0)

    def gather_start(g):
        mine = ag.at[g, c, chip]

        def send(zz, yy, is_me):
            @pl.when(active(g, zz))
            def _():
                if is_me:
                    pltpu.make_async_copy(own.at[g], mine, ag_recv.at[g, zme]).start()
                else:
                    pltpu.make_async_remote_copy(
                        own.at[g], mine, ag_send.at[g], ag_recv.at[g, zme], at_chip(zz * NY + yy)
                    ).start()

        peers(FAR_FIRST, send)

    def gather_forward(g):
        for dz in NEAR_FIRST:
            zz = lax.rem(zme + dz, NZ)
            four = ag.at[g, c, pl.ds(zz * NY, NY)]
            pltpu.make_async_copy(four, four, ag_recv.at[g, zz]).wait()
            pltpu.make_async_remote_copy(four, four, fw_send.at[g], fw_recv.at[g, zz], {"tok": mate}).start()

    def gather_finish(g):
        for z in range(NZ):
            four = ag.at[g, 1 - c, pl.ds(z * NY, NY)]
            pltpu.make_async_copy(four, four, fw_recv.at[g, z]).wait()
            block = ag[g, :, z * NY : (z + 1) * NY].reshape(NC * NY * SLOT, HD)
            ordered = nn(perm[...], block)
            for m in range(3):
                nat[m, z * ZROWS : (z + 1) * ZROWS] = ordered[m * ZROWS : (m + 1) * ZROWS]
        gt[...] = nat[0].astype(BF16)
        ut[...] = nat[1].astype(BF16)
        dt[...] = nat[2].astype(BF16)

    def gather_drain(g):
        sends = NY * (LAST_FIRST if g == 0 else NZ - FIRST_SECOND)

        def drain(n):
            some = ag.at[g, 0, pl.ds(0, n)]
            pltpu.make_async_copy(some, some, ag_send.at[g]).wait()

        @pl.when(live[g])
        def _():
            drain(sends - 1)
            every = ag.at[g, 0]
            pltpu.make_async_copy(every, every, fw_send.at[g]).wait()

        @pl.when(jnp.logical_not(live[g]))
        def _():
            drain(sends)

    def grads(g):
        kk, e = k[...], es[g]
        a = nn(gt[...], kk)
        b = nn(ut[...], kk)
        s = jax.nn.sigmoid(a)
        act = a * s
        r = (act * b).astype(BF16)
        du = tn(dt[...], e)
        da = (du * b * s * (1.0 + a * (1.0 - s))).astype(BF16)
        db = (du * act).astype(BF16)
        nat[0] = nt(da, kk)
        nat[1] = nt(db, kk)
        nat[2] = nt(e, r)

    def reduce_start(g):
        for z in range(NZ):
            part = [nat[m, z * ZROWS : (z + 1) * ZROWS] for m in range(3)]
            part.append(jnp.zeros((128 - 3 * ZROWS, HD), F32))
            block = nn(perm_t[...], jnp.concatenate(part, axis=0).astype(BF16)).astype(BF16)
            gs[g, :, z * NY : (z + 1) * NY] = block.reshape(NC, NY, SLOT, HD)
            pltpu.make_async_remote_copy(
                gs.at[g, 1 - c, pl.ds(z * NY, NY)], cr.at[g, pl.ds(z * NY, NY)],
                cs_send.at[g], cs_recv.at[g, z], {"tok": mate},
            ).start()
        for dz in FAR_FIRST:
            zz = lax.rem(zme + dz, NZ)
            here = pl.ds(zz * NY, NY)
            four = cr.at[g, here]
            pltpu.make_async_copy(four, four, cs_recv.at[g, zz]).wait()
            red[g, here] = (gs[g, c, here].astype(F32) + cr[g, here].astype(F32)).astype(BF16)
            landing = rr.at[g, chip - z_from[g] * NY]

            def send(z_to, yy, is_me):
                p = z_to * NY + yy
                if is_me:
                    pltpu.make_async_copy(red.at[g, p], landing, rs_recv.at[g]).start()
                else:
                    pltpu.make_async_remote_copy(
                        red.at[g, p], landing, rs_send.at[g], rs_recv.at[g], at_chip(p)
                    ).start()

            peers((dz,), send)

    def reduce_finish(g):
        every = rr.at[g]
        pltpu.make_async_copy(every, every, rs_recv.at[g]).wait()
        total = jnp.sum(rr[g].astype(F32), axis=0)
        old = state[...]
        fresh = old - total
        old_norm = jnp.sqrt(jnp.sum(old * old, axis=1, keepdims=True))
        new_norm = jnp.sqrt(jnp.sum(fresh * fresh, axis=1, keepdims=True) + 1e-06)
        return fresh * (old_norm / new_norm)

    def reduce_drain(g):
        @pl.when(live[g])
        def _():
            every = cr.at[g]
            pltpu.make_async_copy(every, every, cs_send.at[g]).wait()
            thirty_one = red.at[g, pl.ds(0, CHIPS - 1)]
            pltpu.make_async_copy(thirty_one, thirty_one, rs_send.at[g]).wait()

    def apply_queries():
        a = nn(gt[...], q[...])
        b = nn(ut[...], q[...])
        hidden = (a * jax.nn.sigmoid(a) * b).astype(BF16)
        return nn(dt[...], hidden)

    def far_copy(n):
        return pltpu.make_async_remote_copy(
            (k, v)[n], kv_far.at[n], kv_send.at[n], kv_recv.at[n], at_chip(lax.rem(chip + 1, CHIPS))
        )

    def near_copy(n, src):
        return pltpu.make_async_remote_copy(src, kv_near.at[n], kv_send.at[2 + n], kv_recv.at[2 + n], {"tok": mate})

    def pass_on(n):
        far_copy(n).wait()

        @pl.when(c == 1)
        def _():
            near_copy(n, kv_far.at[n]).start()

    gather_start(0)

    @pl.when(c == 0)
    def _():
        for n in range(2):
            near_copy(n, (k, v)[n]).start()

    @pl.when(live[0])
    def _():
        gather_forward(0)

    far_copy(0).start()

    @pl.when(live[0])
    def _():
        gather_finish(0)
        grads(0)
        reduce_start(0)
        y_buf[...] = apply_queries()

    pass_on(0)
    middle = reduce_finish(0)
    state[...] = middle
    own[1] = middle.astype(BF16)
    gather_start(1)

    near_copy(0, k).wait()
    scale = 1.0 / math.sqrt(HD)
    j = lax.broadcasted_iota(jnp.int32, (toks, toks), 0)
    i = lax.broadcasted_iota(jnp.int32, (toks, toks), 1)
    reach = back[...]
    scores = []
    for ahead, keys in ((2 * toks, kv_far.at[0]), (toks, kv_near.at[0]), (0, k)):
        away = i - j + ahead
        seen = (away >= 0) & (away <= reach) & (start + j - ahead >= 0)
        scores.append(jnp.where(seen, tn(keys[...], q[...]) * scale, -jnp.inf))
    top = functools.reduce(jnp.maximum, [jnp.max(s, axis=0, keepdims=True) for s in scores])
    weights = [jnp.exp(s - top) for s in scores]
    total = functools.reduce(jnp.add, [jnp.sum(w, axis=0, keepdims=True) for w in weights])
    for n, w in enumerate(weights):
        probs[n] = (w / total).astype(BF16)

    @pl.when(live[1])
    def _():
        gather_forward(1)

    far_copy(1).start()

    @pl.when(live[1])
    def _():
        gather_finish(1)
        grads(1)
        reduce_start(1)
        y_buf[...] = jnp.where(first, y_buf[...], apply_queries())

    mixed = y_buf[...]
    sums = jnp.sum(mixed * mixed, axis=0, keepdims=True)
    sq[...] = sums
    sqr[h] = sums

    def send_squares(n, _):
        pltpu.make_async_remote_copy(sq, sqr.at[h], sq_send, sq_recv, {"head": lax.rem(h + n, HEADS)}).start()
        return 0

    lax.fori_loop(1, HEADS, send_squares, 0)
    pass_on(1)
    near_copy(1, v).wait()
    attn = nn(kv_far[1], probs[0]) + nn(kv_near[1], probs[1]) + nn(v[...], probs[2])
    seven = sqr.at[pl.ds(0, HEADS - 1)]
    pltpu.make_async_copy(seven, seven, sq_recv).wait()
    mean_square = jnp.sum(sqr[...], axis=0) / (HEADS * HD)
    gains = jnp.broadcast_to(gain[...].reshape(1, HD), (8, HD)).T[:, 0:1]
    normed = y_buf[...] / jnp.sqrt(mean_square + 1e-06) * gains
    out[...] = (normed + attn).astype(BF16)
    last = reduce_finish(1)
    for m, ref in enumerate((g_out, u_out, d_out)):
        ref[...] = last[m * OWN : (m + 1) * OWN].reshape(OWN, 1, HD)
    pltpu.make_async_copy(seven, seven, sq_send).wait()
    for g in range(2):
        gather_drain(g)
        reduce_drain(g)


def on_device(queries, keys, values, rates, back, group_end, gate_init, up_init, down_init, gain):
    toks = rates.shape[0]
    perm = order_matrix()
    vmem = pl.BlockSpec(memory_space=pltpu.VMEM)
    anywhere = pl.BlockSpec(memory_space=pl.ANY)
    slots = (CHIPS, SLOT, HD)
    dma = pltpu.SemaphoreType.DMA
    shares = [w.transpose(2, 0, 1) for w in (gate_init, up_init, down_init)]
    share = jax.ShapeDtypeStruct((OWN, 1, HD), F32)
    out, *finals = pl.pallas_call(
        kernel,
        out_shape=(jax.ShapeDtypeStruct((HD, toks), BF16), share, share, share),
        in_specs=[pl.BlockSpec(memory_space=pltpu.SMEM)] + [anywhere] * 9 + [vmem] * 2,
        out_specs=(vmem,) * 4,
        scratch_shapes=[
            pltpu.VMEM((HD, toks), BF16),
            pltpu.VMEM((HD, toks), BF16),
            pltpu.VMEM((HD, toks), BF16),
            pltpu.VMEM((1, toks), F32),
            pltpu.VMEM((1, toks), jnp.int32),
            pltpu.VMEM((SLOT, 1, HD), F32),
            pltpu.VMEM((HD,), F32),
            pltpu.VMEM((2, SLOT, HD), BF16),
            pltpu.VMEM((2, NC, *slots), BF16),
            pltpu.VMEM((2, NC, *slots), BF16),
            pltpu.VMEM((2, *slots), BF16),
            pltpu.VMEM((2, *slots), BF16),
            pltpu.VMEM((2, LAST_FIRST * NY, SLOT, HD), BF16),
            pltpu.VMEM((2, HD, toks), BF16),
            pltpu.VMEM((2, HD, toks), BF16),
            pltpu.VMEM((1, toks), F32),
            pltpu.VMEM((HEADS, 1, toks), F32),
            pltpu.VMEM((3, HD, HD), F32),
            pltpu.VMEM((FH, HD), BF16),
            pltpu.VMEM((FH, HD), BF16),
            pltpu.VMEM((HD, FH), BF16),
            pltpu.VMEM((2, HD, toks), BF16),
            pltpu.VMEM((HD, toks), F32),
            pltpu.VMEM((3, toks, toks), BF16),
            pltpu.VMEM((SLOT, HD), F32),
            dma((9,)),
            dma((2,)), dma((2, NZ)),
            dma((2,)), dma((2, NZ)),
            dma((2,)), dma((2, NZ)),
            dma((2,)), dma((2,)),
            dma((4,)), dma((4,)),
            dma, dma,
        ],
        compiler_params=pltpu.CompilerParams(
            collective_id=0, has_side_effects=True, vmem_limit_bytes=48 * 1024 * 1024
        ),
        name="layer",
    )(
        group_end, queries.T, keys.T, values.T, rates.T, back.reshape(1, toks), *shares, gain,
        jnp.asarray(perm, BF16), jnp.asarray(perm.T, BF16),
    )
    return (out.T, *(w.transpose(1, 2, 0) for w in finals))


def solution(mesh):
    placed = (
        P("tok", "head"),
        P("tok", "head"),
        P("tok", "head"),
        P("tok", "head"),
        P("tok"),
        P(),
        P("head", None, "tok"),
        P("head", None, "tok"),
        P("head", None, "tok"),
        P("head"),
    )
    return jax.shard_map(
        on_device,
        mesh=mesh,
        in_specs=placed,
        out_specs=(
            P("tok", "head"),
            P("head", None, "tok"),
            P("head", None, "tok"),
            P("head", None, "tok"),
        ),
        check_vma=False,
    )
```

time: 92.8 us -> 86.4 us (0.931)
  Pallas kernels: 82.7 us -> 75.2 us
  local copies, waits for them, and re-layouts: 8.07 us -> 9.45 us
    pallas_call x1, Pallas kernels: 82.7 us -> 75.2 us  [on_device(): pl.pallas_call(kernel, out_shape=(jax.ShapeDtypeStruct((HD, toks), BF16),...]
    unnamed x29 -> x26, local copies, waits for them, and re-layouts: 7.18 us -> 9.45 us
where the time goes in v2:
time: 86.4 us; the launch traced here: 86 us
  Pallas kernels  75.2 us (87%)
  local copies, waits for them, and re-layouts  9.45 us (11%)
  between operations  1.34 us (2%)
    pallas_call x1, Pallas kernels, on_device(): pl.pallas_call(kernel, out_shape=(jax.ShapeDtypeStruct((HD, toks), BF16),...  75.2 us
    unnamed x26, local copies, waits for them, and re-layouts  9.45 us

profile of v2, /device:TPU:1, one launch (start us, length us, event | category | flops | bytes accessed | tf_op | source)
XLA Modules:
  0.0 86.0 jit_solution(17110696221881133553)
XLA Ops:
  0.6 0.0 copy-start.8
  1.3 0.0 copy-start.5
  1.3 0.0 copy-start.6
  1.3 0.0 copy-done.8
  1.3 0.7 copy-done.5
  2.0 0.0 copy-done.6
  2.0 0.0 copy-start
  2.0 0.9 %copy-done = bf16[256,320]{0,1:T(8,128)(2,1)S(1)} copy-done((bf16[256,320]{0,1:T(8,128)(2,1)S(1)}, bf16[256,320]{0,1:T(8,128)(2,1)}, u32[]{:S(2)}) %copy-start) | copy-done | bytes 163864
  2.9 0.0 copy-start.1
  2.9 0.9 %copy-done.1 = bf16[256,320]{0,1:T(8,128)(2,1)S(1)} copy-done((bf16[256,320]{0,1:T(8,128)(2,1)S(1)}, bf16[256,320]{0,1:T(8,128)(2,1)}, u32[]{:S(2)}) %copy-start.1) | copy-done | bytes 163864
  3.8 0.0 copy-start.2
  3.9 0.9 %copy-done.2 = bf16[256,320]{0,1:T(8,128)(2,1)S(1)} copy-done((bf16[256,320]{0,1:T(8,128)(2,1)S(1)}, bf16[256,320]{0,1:T(8,128)(2,1)}, u32[]{:S(2)}) %copy-start.2) | copy-done | bytes 163864
  4.8 0.0 copy-start.3
  4.8 0.8 copy-done.3
  5.5 0.0 copy-start.4
  5.5 0.8 copy-done.4
  6.3 0.0 copy-start.7
  6.3 0.7 copy-done.7
  7.0 0.0 copy-start.9
  7.0 0.7 copy-done.9
  7.7 0.0 copy-start.10
  7.7 0.7 copy-done.10
  8.3 75.2 %layer.1 = (bf16[320,256]{1,0:T(8,128)(2,1)S(1)}, f32[5,1,320]{2,1,0:T(1,128)S(1)}, f32[5,1,320]{2,1,0:T(1,128)S(1)}, f32[5,1,320]{2,1,0:T(1,128)S(1)}) custom-call(s32[1]{0:T(128)S(6)} %copy.20.ge, bf16[320,256]{1,0:T(8,128)(2,1)S(1)} %bitcast.13, bf16[320,256]{1,0:T(8,128)(2,1)S(1)} %bitcast.14, bf16[320,256]{1,0:T(8,128)(2,1)S(1)} %bitcast.15, ...), custom_call_target="tpu_custom_call" | custom-call | tf_op jit(solution)/shard_map/layer/pallas_call | solution.py:356
  83.5 0.7 copy.21
  84.2 0.6 copy.22
  84.8 0.6 copy.23
  85.4 0.6 copy.24
Async XLA Ops:
  0.6 0.7 copy-start.8
  1.3 0.7 copy-start.5
  1.3 0.7 copy-start.6
  2.0 0.9 %copy-start = (bf16[256,320]{0,1:T(8,128)(2,1)S(1)}, bf16[256,320]{0,1:T(8,128)(2,1)}, u32[]{:S(2)}) copy-start(bf16[256,320]{0,1:T(8,128)(2,1)} %param.12) | copy-start | bytes 491524
  2.9 0.9 %copy-start.1 = (bf16[256,320]{0,1:T(8,128)(2,1)S(1)}, bf16[256,320]{0,1:T(8,128)(2,1)}, u32[]{:S(2)}) copy-start(bf16[256,320]{0,1:T(8,128)(2,1)} %param.13) | copy-start | bytes 491524
  3.8 0.9 %copy-start.2 = (bf16[256,320]{0,1:T(8,128)(2,1)S(1)}, bf16[256,320]{0,1:T(8,128)(2,1)}, u32[]{:S(2)}) copy-start(bf16[256,320]{0,1:T(8,128)(2,1)} %param.14) | copy-start | bytes 491524
  4.8 0.8 copy-start.3
  5.5 0.8 copy-start.4
  6.3 0.7 copy-start.7
  7.0 0.7 copy-start.9
  7.7 0.7 copy-start.10

commit v3 on v2

--- a/solution.py
+++ b/solution.py
@@ -48,9 +48,9 @@
 
 
 def kernel(
-    ge, q_hbm, k_hbm, v_hbm, rates_hbm, back_hbm, g_hbm, u_hbm, d_hbm, gain_hbm, perm, perm_t,
+    ge, q_hbm, k_hbm, v_hbm, rates_hbm, back_hbm, g_hbm, u_hbm, d_hbm, gain_hbm, perm_hbm, perm_t_hbm,
     out, g_out, u_out, d_out,
-    q, k, v, rates, back, rows0, gain,
+    q, k, v, rates, back, rows0, gain, perm, perm_t,
     own, ag, gs, cr, red, rr, kv_far, kv_near, sq, sqr, nat, gt, ut, dt, es, y_buf, probs, state,
     in_sem, ag_send, ag_recv, fw_send, fw_recv, cs_send, cs_recv, rs_send, rs_recv, kv_send, kv_recv, sq_send, sq_recv,
 ):
@@ -76,6 +76,8 @@
                 (rates_hbm, rates),
                 (back_hbm, back),
                 (gain_hbm, gain),
+                (perm_hbm, perm),
+                (perm_t_hbm, perm_t),
             )
         )
     ]
@@ -344,19 +346,30 @@
         reduce_drain(g)
 
 
+def write_out(*refs):
+    half = len(refs) // 2
+    srcs, dsts, sem = refs[:half], refs[half:-1], refs[-1]
+    copies = [pltpu.make_async_copy(src, dst, sem.at[n]) for n, (src, dst) in enumerate(zip(srcs, dsts))]
+    for copy in copies:
+        copy.start()
+    for copy in copies:
+        copy.wait()
+
+
 def on_device(queries, keys, values, rates, back, group_end, gate_init, up_init, down_init, gain):
     toks = rates.shape[0]
     perm = order_matrix()
     vmem = pl.BlockSpec(memory_space=pltpu.VMEM)
-    anywhere = pl.BlockSpec(memory_space=pl.ANY)
+    hbm = pl.BlockSpec(memory_space=pltpu.HBM)
     slots = (CHIPS, SLOT, HD)
     dma = pltpu.SemaphoreType.DMA
     shares = [w.transpose(2, 0, 1) for w in (gate_init, up_init, down_init)]
     share = jax.ShapeDtypeStruct((OWN, 1, HD), F32)
-    out, *finals = pl.pallas_call(
+    shapes = (jax.ShapeDtypeStruct((HD, toks), BF16), share, share, share)
+    results = pl.pallas_call(
         kernel,
-        out_shape=(jax.ShapeDtypeStruct((HD, toks), BF16), share, share, share),
-        in_specs=[pl.BlockSpec(memory_space=pltpu.SMEM)] + [anywhere] * 9 + [vmem] * 2,
+        out_shape=shapes,
+        in_specs=[pl.BlockSpec(memory_space=pltpu.SMEM)] + [hbm] * 11,
         out_specs=(vmem,) * 4,
         scratch_shapes=[
             pltpu.VMEM((HD, toks), BF16),
@@ -366,6 +379,8 @@
             pltpu.VMEM((1, toks), jnp.int32),
             pltpu.VMEM((SLOT, 1, HD), F32),
             pltpu.VMEM((HD,), F32),
+            pltpu.VMEM((128, 128), BF16),
+            pltpu.VMEM((128, 128), BF16),
             pltpu.VMEM((2, SLOT, HD), BF16),
             pltpu.VMEM((2, NC, *slots), BF16),
             pltpu.VMEM((2, NC, *slots), BF16),
@@ -384,7 +399,7 @@
             pltpu.VMEM((HD, toks), F32),
             pltpu.VMEM((3, toks, toks), BF16),
             pltpu.VMEM((SLOT, HD), F32),
-            dma((9,)),
+            dma((11,)),
             dma((2,)), dma((2, NZ)),
             dma((2,)), dma((2, NZ)),
             dma((2,)), dma((2, NZ)),
@@ -397,9 +412,24 @@
         ),
         name="layer",
     )(
-        group_end, queries.T, keys.T, values.T, rates.T, back.reshape(1, toks), *shares, gain,
-        jnp.asarray(perm, BF16), jnp.asarray(perm.T, BF16),
+        group_end,
+        *(
+            pltpu.with_memory_space_constraint(array, pltpu.HBM)
+            for array in (
+                queries.T, keys.T, values.T, rates.T, back.reshape(1, toks), *shares, gain,
+                jnp.asarray(perm, BF16), jnp.asarray(perm.T, BF16),
+            )
+        ),
     )
+    out, *finals = pl.pallas_call(
+        write_out,
+        out_shape=shapes,
+        in_specs=[vmem] * 4,
+        out_specs=(hbm,) * 4,
+        scratch_shapes=[dma((4,))],
+        compiler_params=pltpu.CompilerParams(vmem_limit_bytes=1024 * 1024),
+        name="write_out",
+    )(*results)
     return (out.T, *(w.transpose(1, 2, 0) for w in finals))
 
 

time: 86.4 us -> 76.7 us (0.89)
  local copies, waits for them, and re-layouts: 9.45 us -> 0 us
    unnamed x26 -> x0, local copies, waits for them, and re-layouts: 9.45 us -> none
    pallas_call x1 -> x2, Pallas kernels: 75.2 us -> 75.3 us  [the longest x1 74.5 us: on_device(): pl.pallas_call(kernel, out_shape=shapes, in_specs=[pl.BlockSpec(memory_sp...]
where the time goes in v3:
time: 76.7 us; the launch traced here: 76.5 us
  Pallas kernels  75.3 us (98%)
  between operations  1.29 us (2%)
    pallas_call x1, Pallas kernels, on_device(): pl.pallas_call(kernel, out_shape=shapes, in_specs=[pl.BlockSpec(memory_sp...  74.5 us

profile of v3, /device:TPU:1, one launch (start us, length us, event | category | flops | bytes accessed | tf_op | source)
XLA Modules:
  0.0 76.5 jit_solution(2619808742557090202)
XLA Ops:
  1.3 74.5 %layer.1 = (bf16[320,256]{1,0:T(8,128)(2,1)S(1)}, f32[5,1,320]{2,1,0:T(1,128)S(1)}, f32[5,1,320]{2,1,0:T(1,128)S(1)}, f32[5,1,320]{2,1,0:T(1,128)S(1)}) custom-call(s32[1]{0:T(128)S(6)} %copy.16.ge, bf16[320,256]{1,0:T(8,128)(2,1)} %bitcast.12, bf16[320,256]{1,0:T(8,128)(2,1)} %bitcast.13, bf16[320,256]{1,0:T(8,128)(2,1)} %bitcast.14, f32[1,256]{1,0:T(1,128)} %bitcast.18, ...), custom_call_target="tpu_custom_call" | custom-call | tf_op jit(solution)/shard_map/layer/pallas_call | solution.py:369
  75.8 0.7 write_out.1

commit v4 on v3

--- a/solution.py
+++ b/solution.py
@@ -17,6 +17,8 @@
 CHIPS = NZ * NY
 OWN = 5
 SLOT = 16
+LINES = 40
+PAD = 384
 ZROWS = NY * NC * OWN
 LAST_FIRST = 12288 * NZ // 16384
 FIRST_SECOND = 4096 * NZ // 16384
@@ -37,20 +39,47 @@
     return lax.dot_general(a, b, (((0,), (0,)), ((), ())), preferred_element_type=F32)
 
 
-def order_matrix():
-    perm = np.zeros((128, 128), np.float32)
+def order_matrices():
+    perm = np.zeros((2, 128, 128), np.float32)
     for m in range(3):
         for y in range(NY):
             for c in range(NC):
                 for j in range(OWN):
-                    perm[m * ZROWS + (y * NC + c) * OWN + j, c * 64 + y * SLOT + m * OWN + j] = 1.0
-    return perm
+                    row = m * OWN + j
+                    natural = m * ZROWS + (y * NC + c) * OWN + j
+                    perm[0, natural, c * 64 + y * SLOT + row] = 1.0
+                    perm[1, natural, row // 8 * 64 + c * 32 + y * 8 + row % 8] = 1.0
+    return np.concatenate([perm, perm.transpose(0, 2, 1)])
+
+
+def pack(rows):
+    last = rows[:, 256:384]
+    return jnp.concatenate([rows[:, 0:128], rows[:, 128:256], last[0:8] + pltpu.roll(last[8:16], 64, 1)], axis=0)
+
+
+def unpack(packed):
+    last = jnp.concatenate([packed[32:40], pltpu.roll(packed[32:40], 64, 1)], axis=0)
+    return jnp.concatenate([packed[0:16], packed[16:32], last[:, 0:64]], axis=1)
+
+
+def row_sums(packed):
+    left = lax.broadcasted_iota(jnp.int32, (8, 128), 1) < 64
+    last = packed[32:40]
+    ends = [jnp.where(left, last, 0.0), jnp.where(left, 0.0, last)]
+    whole = packed[0:16] + packed[16:32] + jnp.concatenate(ends, axis=0)
+    return jnp.sum(whole, axis=1, keepdims=True)
+
+
+def spread(factor):
+    wide = jnp.broadcast_to(factor, (SLOT, 128))
+    left = lax.broadcasted_iota(jnp.int32, (8, 128), 1) < 64
+    return jnp.concatenate([wide, wide, jnp.where(left, wide[0:8], wide[8:16])], axis=0)
 
 
 def kernel(
-    ge, q_hbm, k_hbm, v_hbm, rates_hbm, back_hbm, g_hbm, u_hbm, d_hbm, gain_hbm, perm_hbm, perm_t_hbm,
+    ge, q_hbm, k_hbm, v_hbm, rates_hbm, back_hbm, g_hbm, u_hbm, d_hbm, gain_hbm, perm_hbm,
     out, g_out, u_out, d_out,
-    q, k, v, rates, back, rows0, gain, perm, perm_t,
+    q, k, v, rates, back, rows0, gain, perm,
     own, ag, gs, cr, red, rr, kv_far, kv_near, sq, sqr, nat, gt, ut, dt, es, y_buf, probs, state,
     in_sem, ag_send, ag_recv, fw_send, fw_recv, cs_send, cs_recv, rs_send, rs_recv, kv_send, kv_recv, sq_send, sq_recv,
 ):
@@ -70,14 +99,13 @@
                 (g_hbm, rows0.at[pl.ds(0, OWN)]),
                 (u_hbm, rows0.at[pl.ds(OWN, OWN)]),
                 (d_hbm, rows0.at[pl.ds(2 * OWN, OWN)]),
-                (k_hbm, k),
+                (k_hbm, k.at[pl.ds(0, HD)]),
                 (v_hbm, v),
                 (q_hbm, q),
                 (rates_hbm, rates),
                 (back_hbm, back),
                 (gain_hbm, gain),
                 (perm_hbm, perm),
-                (perm_t_hbm, perm_t),
             )
         )
     ]
@@ -105,8 +133,10 @@
     rows0[pl.ds(3 * OWN, 1)] = jnp.zeros((1, 1, HD), F32)
     for load in loads:
         load.wait()
-    state[...] = rows0[...].reshape(SLOT, HD)
+    share = rows0[...].reshape(SLOT, HD)
+    state[...] = pack(jnp.concatenate([share, jnp.zeros((SLOT, PAD - HD), F32)], axis=1))
     own[0] = state[...].astype(BF16)
+    k[pl.ds(HD, PAD - HD)] = jnp.zeros((PAD - HD, toks), BF16)
     start = t * toks
     first = start + lax.broadcasted_iota(jnp.int32, (1, toks), 1) < ge[0]
     rate = rates[...]
@@ -145,24 +175,38 @@
 
         peers(FAR_FIRST, send)
 
-    def gather_forward(g):
-        for dz in NEAR_FIRST:
-            zz = lax.rem(zme + dz, NZ)
+    def block_at(zz):
+        return pl.ds(pl.multiple_of(zz * ZROWS, 8), ZROWS)
+
+    def gather_finish(g):
+        def arrange(zz):
+            four = ag.at[g, 1 - c, pl.ds(zz * NY, NY)]
+            pltpu.make_async_copy(four, four, fw_recv.at[g, zz]).wait()
+            both = [ag[g, core, pl.ds(zz * NY, NY)] for core in range(NC)]
+            wide = [
+                jnp.concatenate([x[:, r : r + SLOT].reshape(NY * SLOT, 128) for x in both], axis=0) for r in (0, SLOT)
+            ]
+            ordered = nn(perm[0], jnp.concatenate(wide, axis=1))
+            ends = jnp.concatenate([x[:, 2 * SLOT :].reshape(NY * 8, 128) for x in both], axis=0).astype(F32)
+            left = lax.broadcasted_iota(jnp.int32, ends.shape, 1) < 64
+            halves = [jnp.where(left, x, 0.0) for x in (ends, pltpu.roll(ends, 64, 1))]
+            ordered_ends = nn(perm[1], jnp.concatenate(halves, axis=0).astype(BF16))
+            for m in range(3):
+                rows = slice(m * ZROWS, (m + 1) * ZROWS)
+                nat[m, block_at(zz), 0:256] = ordered[rows]
+                nat[m, block_at(zz), 256:PAD] = ordered_ends[rows]
+
+        order = [lax.rem(zme + dz, NZ) for dz in NEAR_FIRST]
+        for n, zz in enumerate(order):
             four = ag.at[g, c, pl.ds(zz * NY, NY)]
             pltpu.make_async_copy(four, four, ag_recv.at[g, zz]).wait()
             pltpu.make_async_remote_copy(four, four, fw_send.at[g], fw_recv.at[g, zz], {"tok": mate}).start()
-
-    def gather_finish(g):
-        for z in range(NZ):
-            four = ag.at[g, 1 - c, pl.ds(z * NY, NY)]
-            pltpu.make_async_copy(four, four, fw_recv.at[g, z]).wait()
-            block = ag[g, :, z * NY : (z + 1) * NY].reshape(NC * NY * SLOT, HD)
-            ordered = nn(perm[...], block)
-            for m in range(3):
-                nat[m, z * ZROWS : (z + 1) * ZROWS] = ordered[m * ZROWS : (m + 1) * ZROWS]
-        gt[...] = nat[0].astype(BF16)
-        ut[...] = nat[1].astype(BF16)
-        dt[...] = nat[2].astype(BF16)
+            if n:
+                arrange(order[n - 1])
+        far_copy(g).start()
+        arrange(order[-1])
+        for m, ref in enumerate((gt, ut, dt)):
+            ref[...] = nat[m, :, 0:HD].astype(BF16)
 
     def gather_drain(g):
         sends = NY * (LAST_FIRST if g == 0 else NZ - FIRST_SECOND)
@@ -182,7 +226,7 @@
             drain(sends)
 
     def grads(g):
-        kk, e = k[...], es[g]
+        kk, e = k[pl.ds(0, HD)], es[g]
         a = nn(gt[...], kk)
         b = nn(ut[...], kk)
         s = jax.nn.sigmoid(a)
@@ -191,38 +235,52 @@
         du = tn(dt[...], e)
         da = (du * b * s * (1.0 + a * (1.0 - s))).astype(BF16)
         db = (du * act).astype(BF16)
-        nat[0] = nt(da, kk)
-        nat[1] = nt(db, kk)
-        nat[2] = nt(e, r)
+        nat[0] = nt(da, k[...])
+        nat[1] = nt(db, k[...])
+        nat[2] = nt(e, jnp.concatenate([r, jnp.zeros((PAD - FH, toks), BF16)], axis=0))
 
     def reduce_start(g):
-        for z in range(NZ):
-            part = [nat[m, z * ZROWS : (z + 1) * ZROWS] for m in range(3)]
-            part.append(jnp.zeros((128 - 3 * ZROWS, HD), F32))
-            block = nn(perm_t[...], jnp.concatenate(part, axis=0).astype(BF16)).astype(BF16)
-            gs[g, :, z * NY : (z + 1) * NY] = block.reshape(NC, NY, SLOT, HD)
+        def split(zz):
+            part = [nat[m, block_at(zz)] for m in range(3)]
+            part.append(jnp.zeros((128 - 3 * ZROWS, PAD), F32))
+            block = jnp.concatenate(part, axis=0).astype(BF16)
+            slots = nn(perm[2], block[:, 0:256]).astype(BF16)
+            ends = nn(perm[3], block[:, 256:PAD])
+            ends = (ends[0:64] + pltpu.roll(ends[64:128], 64, 1)).astype(BF16)
+            here = pl.ds(zz * NY, NY)
+            gs[g, :, here, 0:SLOT] = slots[:, 0:128].reshape(NC, NY, SLOT, 128)
+            gs[g, :, here, SLOT : 2 * SLOT] = slots[:, 128:256].reshape(NC, NY, SLOT, 128)
+            gs[g, :, here, 2 * SLOT : LINES] = ends.reshape(NC, NY, 8, 128)
             pltpu.make_async_remote_copy(
-                gs.at[g, 1 - c, pl.ds(z * NY, NY)], cr.at[g, pl.ds(z * NY, NY)],
-                cs_send.at[g], cs_recv.at[g, z], {"tok": mate},
+                gs.at[g, 1 - c, here], cr.at[g, here], cs_send.at[g], cs_recv.at[g, zz], {"tok": mate}
             ).start()
-        for dz in FAR_FIRST:
+
+        landing = rr.at[g, chip - z_from[g] * NY]
+
+        def send(zz, yy, is_me):
+            p = zz * NY + yy
+            if is_me:
+                pltpu.make_async_copy(red.at[g, p], landing, rs_recv.at[g]).start()
+            else:
+                pltpu.make_async_remote_copy(
+                    red.at[g, p], landing, rs_send.at[g], rs_recv.at[g], at_chip(p)
+                ).start()
+
+        def pass_sum(dz):
             zz = lax.rem(zme + dz, NZ)
             here = pl.ds(zz * NY, NY)
             four = cr.at[g, here]
             pltpu.make_async_copy(four, four, cs_recv.at[g, zz]).wait()
             red[g, here] = (gs[g, c, here].astype(F32) + cr[g, here].astype(F32)).astype(BF16)
-            landing = rr.at[g, chip - z_from[g] * NY]
-
-            def send(z_to, yy, is_me):
-                p = z_to * NY + yy
-                if is_me:
-                    pltpu.make_async_copy(red.at[g, p], landing, rs_recv.at[g]).start()
-                else:
-                    pltpu.make_async_remote_copy(
-                        red.at[g, p], landing, rs_send.at[g], rs_recv.at[g], at_chip(p)
-                    ).start()
-
             peers((dz,), send)
+
+        lag = 4
+        for n, dz in enumerate(FAR_FIRST):
+            split(lax.rem(zme + dz, NZ))
+            if n >= lag:
+                pass_sum(FAR_FIRST[n - lag])
+        for dz in FAR_FIRST[NZ - lag :]:
+            pass_sum(dz)
 
     def reduce_finish(g):
         every = rr.at[g]
@@ -230,9 +288,9 @@
         total = jnp.sum(rr[g].astype(F32), axis=0)
         old = state[...]
         fresh = old - total
-        old_norm = jnp.sqrt(jnp.sum(old * old, axis=1, keepdims=True))
-        new_norm = jnp.sqrt(jnp.sum(fresh * fresh, axis=1, keepdims=True) + 1e-06)
-        return fresh * (old_norm / new_norm)
+        old_norm = jnp.sqrt(row_sums(old * old))
+        new_norm = jnp.sqrt(row_sums(fresh * fresh) + 1e-06)
+        return fresh * spread(old_norm / new_norm)
 
     def reduce_drain(g):
         @pl.when(live[g])
@@ -250,7 +308,7 @@
 
     def far_copy(n):
         return pltpu.make_async_remote_copy(
-            (k, v)[n], kv_far.at[n], kv_send.at[n], kv_recv.at[n], at_chip(lax.rem(chip + 1, CHIPS))
+            (k.at[pl.ds(0, HD)], v)[n], kv_far.at[n], kv_send.at[n], kv_recv.at[n], at_chip(lax.rem(chip + 1, CHIPS))
         )
 
     def near_copy(n, src):
@@ -268,13 +326,11 @@
     @pl.when(c == 0)
     def _():
         for n in range(2):
-            near_copy(n, (k, v)[n]).start()
-
-    @pl.when(live[0])
+            near_copy(n, (k.at[pl.ds(0, HD)], v)[n]).start()
+
+    @pl.when(jnp.logical_not(live[0]))
     def _():
-        gather_forward(0)
-
-    far_copy(0).start()
+        far_copy(0).start()
 
     @pl.when(live[0])
     def _():
@@ -289,13 +345,13 @@
     own[1] = middle.astype(BF16)
     gather_start(1)
 
-    near_copy(0, k).wait()
+    near_copy(0, kv_far.at[0]).wait()
     scale = 1.0 / math.sqrt(HD)
     j = lax.broadcasted_iota(jnp.int32, (toks, toks), 0)
     i = lax.broadcasted_iota(jnp.int32, (toks, toks), 1)
     reach = back[...]
     scores = []
-    for ahead, keys in ((2 * toks, kv_far.at[0]), (toks, kv_near.at[0]), (0, k)):
+    for ahead, keys in ((2 * toks, kv_far.at[0]), (toks, kv_near.at[0]), (0, k.at[pl.ds(0, HD)])):
         away = i - j + ahead
         seen = (away >= 0) & (away <= reach) & (start + j - ahead >= 0)
         scores.append(jnp.where(seen, tn(keys[...], q[...]) * scale, -jnp.inf))
@@ -305,11 +361,9 @@
     for n, w in enumerate(weights):
         probs[n] = (w / total).astype(BF16)
 
-    @pl.when(live[1])
+    @pl.when(jnp.logical_not(live[1]))
     def _():
-        gather_forward(1)
-
-    far_copy(1).start()
+        far_copy(1).start()
 
     @pl.when(live[1])
     def _():
@@ -337,7 +391,7 @@
     gains = jnp.broadcast_to(gain[...].reshape(1, HD), (8, HD)).T[:, 0:1]
     normed = y_buf[...] / jnp.sqrt(mean_square + 1e-06) * gains
     out[...] = (normed + attn).astype(BF16)
-    last = reduce_finish(1)
+    last = unpack(reduce_finish(1))
     for m, ref in enumerate((g_out, u_out, d_out)):
         ref[...] = last[m * OWN : (m + 1) * OWN].reshape(OWN, 1, HD)
     pltpu.make_async_copy(seven, seven, sq_send).wait()
@@ -358,10 +412,10 @@
 
 def on_device(queries, keys, values, rates, back, group_end, gate_init, up_init, down_init, gain):
     toks = rates.shape[0]
-    perm = order_matrix()
+    perm = order_matrices()
     vmem = pl.BlockSpec(memory_space=pltpu.VMEM)
     hbm = pl.BlockSpec(memory_space=pltpu.HBM)
-    slots = (CHIPS, SLOT, HD)
+    slots = (CHIPS, LINES, 128)
     dma = pltpu.SemaphoreType.DMA
     shares = [w.transpose(2, 0, 1) for w in (gate_init, up_init, down_init)]
     share = jax.ShapeDtypeStruct((OWN, 1, HD), F32)
@@ -369,37 +423,36 @@
     results = pl.pallas_call(
         kernel,
         out_shape=shapes,
-        in_specs=[pl.BlockSpec(memory_space=pltpu.SMEM)] + [hbm] * 11,
+        in_specs=[pl.BlockSpec(memory_space=pltpu.SMEM)] + [hbm] * 10,
         out_specs=(vmem,) * 4,
         scratch_shapes=[
             pltpu.VMEM((HD, toks), BF16),
-            pltpu.VMEM((HD, toks), BF16),
+            pltpu.VMEM((PAD, toks), BF16),
             pltpu.VMEM((HD, toks), BF16),
             pltpu.VMEM((1, toks), F32),
             pltpu.VMEM((1, toks), jnp.int32),
             pltpu.VMEM((SLOT, 1, HD), F32),
             pltpu.VMEM((HD,), F32),
-            pltpu.VMEM((128, 128), BF16),
-            pltpu.VMEM((128, 128), BF16),
-            pltpu.VMEM((2, SLOT, HD), BF16),
+            pltpu.VMEM((4, 128, 128), BF16),
+            pltpu.VMEM((2, LINES, 128), BF16),
             pltpu.VMEM((2, NC, *slots), BF16),
             pltpu.VMEM((2, NC, *slots), BF16),
             pltpu.VMEM((2, *slots), BF16),
             pltpu.VMEM((2, *slots), BF16),
-            pltpu.VMEM((2, LAST_FIRST * NY, SLOT, HD), BF16),
+            pltpu.VMEM((2, LAST_FIRST * NY, LINES, 128), BF16),
             pltpu.VMEM((2, HD, toks), BF16),
             pltpu.VMEM((2, HD, toks), BF16),
             pltpu.VMEM((1, toks), F32),
             pltpu.VMEM((HEADS, 1, toks), F32),
-            pltpu.VMEM((3, HD, HD), F32),
+            pltpu.VMEM((3, HD, PAD), F32),
             pltpu.VMEM((FH, HD), BF16),
             pltpu.VMEM((FH, HD), BF16),
             pltpu.VMEM((HD, FH), BF16),
             pltpu.VMEM((2, HD, toks), BF16),
             pltpu.VMEM((HD, toks), F32),
             pltpu.VMEM((3, toks, toks), BF16),
-            pltpu.VMEM((SLOT, HD), F32),
-            dma((11,)),
+            pltpu.VMEM((LINES, 128), F32),
+            dma((10,)),
             dma((2,)), dma((2, NZ)),
             dma((2,)), dma((2, NZ)),
             dma((2,)), dma((2, NZ)),
@@ -417,7 +470,7 @@
             pltpu.with_memory_space_constraint(array, pltpu.HBM)
             for array in (
                 queries.T, keys.T, values.T, rates.T, back.reshape(1, toks), *shares, gain,
-                jnp.asarray(perm, BF16), jnp.asarray(perm.T, BF16),
+                jnp.asarray(perm, BF16),
             )
         ),
     )

time: 76.7 us -> 76.5 us (level)
  no operation moved by 1% of the time
where the time goes in v4:
time: 76.5 us; the launch traced here: 76.4 us
  Pallas kernels  75.1 us (98%)
  between operations  1.29 us (2%)
    pallas_call x1, Pallas kernels, on_device(): pl.pallas_call(kernel, out_shape=shapes, in_specs=[pl.BlockSpec(memory_sp...  74.4 us

profile of v4, /device:TPU:1, one launch (start us, length us, event | category | flops | bytes accessed | tf_op | source)
XLA Modules:
  0.0 76.4 jit_solution(17386786397043499391)
XLA Ops:
  1.3 74.4 %layer.1 = (bf16[320,256]{1,0:T(8,128)(2,1)S(1)}, f32[5,1,320]{2,1,0:T(1,128)S(1)}, f32[5,1,320]{2,1,0:T(1,128)S(1)}, f32[5,1,320]{2,1,0:T(1,128)S(1)}) custom-call(s32[1]{0:T(128)S(6)} %copy.15.ge, bf16[320,256]{1,0:T(8,128)(2,1)} %bitcast.12, bf16[320,256]{1,0:T(8,128)(2,1)} %bitcast.13, bf16[320,256]{1,0:T(8,128)(2,1)} %bitcast.14, f32[1,256]{1,0:T(1,128)} %bitcast.18, ...), custom_call_target="tpu_custom_call" | custom-call | tf_op jit(solution)/shard_map/layer/pallas_call | solution.py:423
  75.7 0.7 write_out.1

commit v5 on v4

--- a/solution.py
+++ b/solution.py
@@ -179,9 +179,11 @@
         return pl.ds(pl.multiple_of(zz * ZROWS, 8), ZROWS)
 
     def gather_finish(g):
-        def arrange(zz):
+        def forwarded(zz):
             four = ag.at[g, 1 - c, pl.ds(zz * NY, NY)]
             pltpu.make_async_copy(four, four, fw_recv.at[g, zz]).wait()
+
+        def arrange(zz):
             both = [ag[g, core, pl.ds(zz * NY, NY)] for core in range(NC)]
             wide = [
                 jnp.concatenate([x[:, r : r + SLOT].reshape(NY * SLOT, 128) for x in both], axis=0) for r in (0, SLOT)
@@ -201,10 +203,16 @@
             four = ag.at[g, c, pl.ds(zz * NY, NY)]
             pltpu.make_async_copy(four, four, ag_recv.at[g, zz]).wait()
             pltpu.make_async_remote_copy(four, four, fw_send.at[g], fw_recv.at[g, zz], {"tok": mate}).start()
-            if n:
-                arrange(order[n - 1])
+            if n % 2 and n >= 5:
+                for zz in order[n - 5 : n - 3]:
+                    forwarded(zz)
+                for zz in order[n - 5 : n - 3]:
+                    arrange(zz)
         far_copy(g).start()
-        arrange(order[-1])
+        for zz in order[4:]:
+            forwarded(zz)
+        for zz in order[4:]:
+            arrange(zz)
         for m, ref in enumerate((gt, ut, dt)):
             ref[...] = nat[m, :, 0:HD].astype(BF16)
 
@@ -239,7 +247,7 @@
         nat[1] = nt(db, k[...])
         nat[2] = nt(e, jnp.concatenate([r, jnp.zeros((PAD - FH, toks), BF16)], axis=0))
 
-    def reduce_start(g):
+    def reduce_start(g, meanwhile):
         def split(zz):
             part = [nat[m, block_at(zz)] for m in range(3)]
             part.append(jnp.zeros((128 - 3 * ZROWS, PAD), F32))
@@ -251,6 +259,9 @@
             gs[g, :, here, 0:SLOT] = slots[:, 0:128].reshape(NC, NY, SLOT, 128)
             gs[g, :, here, SLOT : 2 * SLOT] = slots[:, 128:256].reshape(NC, NY, SLOT, 128)
             gs[g, :, here, 2 * SLOT : LINES] = ends.reshape(NC, NY, 8, 128)
+
+        def to_mate(zz):
+            here = pl.ds(zz * NY, NY)
             pltpu.make_async_remote_copy(
                 gs.at[g, 1 - c, here], cr.at[g, here], cs_send.at[g], cs_recv.at[g, zz], {"tok": mate}
             ).start()
@@ -274,12 +285,13 @@
             red[g, here] = (gs[g, c, here].astype(F32) + cr[g, here].astype(F32)).astype(BF16)
             peers((dz,), send)
 
-        lag = 4
-        for n, dz in enumerate(FAR_FIRST):
-            split(lax.rem(zme + dz, NZ))
-            if n >= lag:
-                pass_sum(FAR_FIRST[n - lag])
-        for dz in FAR_FIRST[NZ - lag :]:
+        for half in (FAR_FIRST[: NZ // 2], FAR_FIRST[NZ // 2 :]):
+            for dz in half:
+                split(lax.rem(zme + dz, NZ))
+            for dz in half:
+                to_mate(lax.rem(zme + dz, NZ))
+        meanwhile()
+        for dz in FAR_FIRST:
             pass_sum(dz)
 
     def reduce_finish(g):
@@ -321,6 +333,14 @@
         def _():
             near_copy(n, kv_far.at[n]).start()
 
+    def exchange_squares():
+        mixed = y_buf[...]
+        sums = jnp.sum(mixed * mixed, axis=0, keepdims=True)
+        sq[...] = sums
+        sqr[h] = sums
+        for n in range(1, HEADS):
+            pltpu.make_async_remote_copy(sq, sqr.at[h], sq_send, sq_recv, {"head": lax.rem(h + n, HEADS)}).start()
+
     gather_start(0)
 
     @pl.when(c == 0)
@@ -336,7 +356,7 @@
     def _():
         gather_finish(0)
         grads(0)
-        reduce_start(0)
+        reduce_start(0, lambda: None)
         y_buf[...] = apply_queries()
 
     pass_on(0)
@@ -369,19 +389,17 @@
     def _():
         gather_finish(1)
         grads(1)
-        reduce_start(1)
-        y_buf[...] = jnp.where(first, y_buf[...], apply_queries())
-
-    mixed = y_buf[...]
-    sums = jnp.sum(mixed * mixed, axis=0, keepdims=True)
-    sq[...] = sums
-    sqr[h] = sums
-
-    def send_squares(n, _):
-        pltpu.make_async_remote_copy(sq, sqr.at[h], sq_send, sq_recv, {"head": lax.rem(h + n, HEADS)}).start()
-        return 0
-
-    lax.fori_loop(1, HEADS, send_squares, 0)
+
+        def outputs():
+            y_buf[...] = jnp.where(first, y_buf[...], apply_queries())
+            exchange_squares()
+
+        reduce_start(1, outputs)
+
+    @pl.when(jnp.logical_not(live[1]))
+    def _():
+        exchange_squares()
+
     pass_on(1)
     near_copy(1, v).wait()
     attn = nn(kv_far[1], probs[0]) + nn(kv_near[1], probs[1]) + nn(v[...], probs[2])

time: 76.5 us -> 72 us (0.941)
  Pallas kernels: 75.1 us -> 70.5 us
    pallas_call x1, Pallas kernels: 74.4 us -> 69.8 us  [on_device(): pl.pallas_call(kernel, out_shape=shapes, in_specs=[pl.BlockSpec(memory_sp...]
where the time goes in v5:
time: 72 us; the launch traced here: 71.8 us
  Pallas kernels  70.5 us (98%)
  between operations  1.29 us (2%)
    pallas_call x1, Pallas kernels, on_device(): pl.pallas_call(kernel, out_shape=shapes, in_specs=[pl.BlockSpec(memory_sp...  69.8 us

profile of v5, /device:TPU:1, one launch (start us, length us, event | category | flops | bytes accessed | tf_op | source)
XLA Modules:
  0.0 71.8 jit_solution(4642848958465473797)
XLA Ops:
  1.3 69.8 %layer.1 = (bf16[320,256]{1,0:T(8,128)(2,1)S(1)}, f32[5,1,320]{2,1,0:T(1,128)S(1)}, f32[5,1,320]{2,1,0:T(1,128)S(1)}, f32[5,1,320]{2,1,0:T(1,128)S(1)}) custom-call(s32[1]{0:T(128)S(6)} %copy.15.ge, bf16[320,256]{1,0:T(8,128)(2,1)} %bitcast.12, bf16[320,256]{1,0:T(8,128)(2,1)} %bitcast.13, bf16[320,256]{1,0:T(8,128)(2,1)} %bitcast.14, f32[1,256]{1,0:T(1,128)} %bitcast.18, ...), custom_call_target="tpu_custom_call" | custom-call | tf_op jit(solution)/shard_map/layer/pallas_call | solution.py:441
  71.1 0.7 write_out.1

commit v6 on v5

--- a/solution.py
+++ b/solution.py
@@ -81,7 +81,7 @@
     out, g_out, u_out, d_out,
     q, k, v, rates, back, rows0, gain, perm,
     own, ag, gs, cr, red, rr, kv_far, kv_near, sq, sqr, nat, gt, ut, dt, es, y_buf, probs, state,
-    in_sem, ag_send, ag_recv, fw_send, fw_recv, cs_send, cs_recv, rs_send, rs_recv, kv_send, kv_recv, sq_send, sq_recv,
+    in_sem, ag_send, ag_recv, fw_send, fw_recv, cs_send, cs_recv, rs_send, rs_recv, kv_send, kv_recv, sq_send, sq_recv, go,
 ):
     toks = q.shape[1]
     t = lax.axis_index("tok")
@@ -109,9 +109,6 @@
             )
         )
     ]
-    for load in loads:
-        load.start()
-
     def at_chip(p):
         return {"tok": 2 * p + c}
 
@@ -129,6 +126,8 @@
         return 0
 
     lax.fori_loop(1, HEADS, greet_head, 0)
+    for load in loads:
+        load.start()
 
     rows0[pl.ds(3 * OWN, 1)] = jnp.zeros((1, 1, HD), F32)
     for load in loads:
@@ -209,6 +208,12 @@
                 for zz in order[n - 5 : n - 3]:
                     arrange(zz)
         far_copy(g).start()
+        tell, away = ((2, 3), 4) if g == 0 else ((4, 5), -4)
+
+        @pl.when((zme == tell[0]) | (zme == tell[1]))
+        def _():
+            pl.semaphore_signal(go, inc=1, device_id={"tok": t + away * NY * NC})
+
         for zz in order[4:]:
             forwarded(zz)
         for zz in order[4:]:
@@ -348,16 +353,17 @@
         for n in range(2):
             near_copy(n, (k.at[pl.ds(0, HD)], v)[n]).start()
 
-    @pl.when(jnp.logical_not(live[0]))
-    def _():
-        far_copy(0).start()
-
     @pl.when(live[0])
     def _():
         gather_finish(0)
         grads(0)
         reduce_start(0, lambda: None)
         y_buf[...] = apply_queries()
+
+    @pl.when(jnp.logical_not(live[0]))
+    def _():
+        pl.semaphore_wait(go, 1)
+        far_copy(0).start()
 
     pass_on(0)
     middle = reduce_finish(0)
@@ -383,6 +389,7 @@
 
     @pl.when(jnp.logical_not(live[1]))
     def _():
+        pl.semaphore_wait(go, 1)
         far_copy(1).start()
 
     @pl.when(live[1])
@@ -477,6 +484,7 @@
             dma((2,)), dma((2,)),
             dma((4,)), dma((4,)),
             dma, dma,
+            pltpu.SemaphoreType.REGULAR,
         ],
         compiler_params=pltpu.CompilerParams(
             collective_id=0, has_side_effects=True, vmem_limit_bytes=48 * 1024 * 1024

time: 72 us -> 69.7 us (0.968)
  Pallas kernels: 70.5 us -> 68.3 us
    pallas_call x1, Pallas kernels: 69.8 us -> 67.5 us  [on_device(): pl.pallas_call(kernel, out_shape=shapes, in_specs=[pl.BlockSpec(memory_sp...]
where the time goes in v6:
time: 69.7 us; the launch traced here: 69.5 us
  Pallas kernels  68.3 us (98%)
  between operations  1.29 us (2%)
    pallas_call x1, Pallas kernels, on_device(): pl.pallas_call(kernel, out_shape=shapes, in_specs=[pl.BlockSpec(memory_sp...  67.5 us

profile of v6, /device:TPU:1, one launch (start us, length us, event | category | flops | bytes accessed | tf_op | source)
XLA Modules:
  0.0 69.5 jit_solution(1250144465931166087)
XLA Ops:
  1.3 67.5 %layer.1 = (bf16[320,256]{1,0:T(8,128)(2,1)S(1)}, f32[5,1,320]{2,1,0:T(1,128)S(1)}, f32[5,1,320]{2,1,0:T(1,128)S(1)}, f32[5,1,320]{2,1,0:T(1,128)S(1)}) custom-call(s32[1]{0:T(128)S(6)} %copy.15.ge, bf16[320,256]{1,0:T(8,128)(2,1)} %bitcast.12, bf16[320,256]{1,0:T(8,128)(2,1)} %bitcast.13, bf16[320,256]{1,0:T(8,128)(2,1)} %bitcast.14, f32[1,256]{1,0:T(1,128)} %bitcast.18, ...), custom_call_target="tpu_custom_call" | custom-call | tf_op jit(solution)/shard_map/layer/pallas_call | solution.py:448
  68.8 0.7 %write_out.1 = (bf16[320,256]{1,0:T(8,128)(2,1)}, f32[5,1,320]{2,1,0:T(1,128)}, f32[5,1,320]{2,1,0:T(1,128)}, f32[5,1,320]{2,1,0:T(1,128)}) custom-call(bf16[320,256]{1,0:T(8,128)(2,1)S(1)} %get-tuple-element.12.refs_0_, f32[5,1,320]{2,1,0:T(1,128)S(1)} %get-tuple-element.13.refs_1_, f32[5,1,320]{2,1,0:T(1,128)S(1)} %get-tuple-element.14.refs_2_, ...), custom_call_target="tpu_custom_call" | custom-call | tf_op jit(solution)/shard_map/write_out/pallas_call | solution.py:503

commit v7 on v6

--- a/solution.py
+++ b/solution.py
@@ -23,7 +23,7 @@
 LAST_FIRST = 12288 * NZ // 16384
 FIRST_SECOND = 4096 * NZ // 16384
 FAR_FIRST = (4, 3, 5, 2, 6, 1, 7, 0)
-NEAR_FIRST = (0, 1, 7, 2, 6, 3, 5, 4)
+NEAR_FIRST = (6, 2, 0, 1, 7, 5, 3, 4)
 F32, BF16 = jnp.float32, jnp.bfloat16
 
 
@@ -114,18 +114,14 @@
 
     barrier = pltpu.get_barrier_semaphore()
 
-    def greet(i, _):
-        pl.semaphore_signal(barrier, inc=1, device_id=at_chip(lax.rem(chip + i, CHIPS)))
-        return 0
-
-    lax.fori_loop(1, CHIPS, greet, 0)
+    for dz in FAR_FIRST:
+        zz = lax.rem(zme + dz, NZ)
+        for dy in range(NY):
+            if dz or dy:
+                pl.semaphore_signal(barrier, inc=1, device_id=at_chip(zz * NY + lax.rem(yme + dy, NY)))
+    for n in range(1, HEADS):
+        pl.semaphore_signal(barrier, inc=1, device_id={"head": lax.rem(h + n, HEADS)})
     pl.semaphore_signal(barrier, inc=1, device_id={"tok": mate})
-
-    def greet_head(i, _):
-        pl.semaphore_signal(barrier, inc=1, device_id={"head": lax.rem(h + i, HEADS)})
-        return 0
-
-    lax.fori_loop(1, HEADS, greet_head, 0)
     for load in loads:
         load.start()
 
@@ -163,16 +159,41 @@
         mine = ag.at[g, c, chip]
 
         def send(zz, yy, is_me):
-            @pl.when(active(g, zz))
+            if is_me:
+                pltpu.make_async_copy(own.at[g], mine, ag_recv.at[g, zme]).start()
+            else:
+                pltpu.make_async_remote_copy(
+                    own.at[g], mine, ag_send.at[g], ag_recv.at[g, zme], at_chip(zz * NY + yy)
+                ).start()
+
+        peers((2, 6), send)
+        for dz in (1, 7, 0):
+
+            @pl.when(active(g, lax.rem(zme + dz, NZ)))
             def _():
-                if is_me:
-                    pltpu.make_async_copy(own.at[g], mine, ag_recv.at[g, zme]).start()
-                else:
-                    pltpu.make_async_remote_copy(
-                        own.at[g], mine, ag_send.at[g], ag_recv.at[g, zme], at_chip(zz * NY + yy)
-                    ).start()
-
-        peers(FAR_FIRST, send)
+                peers((dz,), send)
+
+    def arrived(g, zz):
+        four = ag.at[g, c, pl.ds(zz * NY, NY)]
+        pltpu.make_async_copy(four, four, ag_recv.at[g, zz]).wait()
+
+    def relay(g, dz):
+        zz = lax.rem(zme + dz, NZ)
+        half = 0 if dz == 6 else NY // 2
+        for more, begin, size in ((1, 0, NY), (2, half, NY // 2)):
+            to = lax.rem(zme + (more if dz == 6 else NZ - more), NZ)
+
+            @pl.when(active(g, to))
+            def _():
+                some = ag.at[g, c, pl.ds(zz * NY + begin, size)]
+                pltpu.make_async_remote_copy(
+                    some, some, ag_send.at[g], ag_recv.at[g, zz], at_chip(to * NY + yme)
+                ).start()
+
+    def relay_only(g):
+        for dz in (2, 6):
+            arrived(g, lax.rem(zme + dz, NZ))
+            relay(g, dz)
 
     def block_at(zz):
         return pl.ds(pl.multiple_of(zz * ZROWS, 8), ZROWS)
@@ -200,7 +221,9 @@
         order = [lax.rem(zme + dz, NZ) for dz in NEAR_FIRST]
         for n, zz in enumerate(order):
             four = ag.at[g, c, pl.ds(zz * NY, NY)]
-            pltpu.make_async_copy(four, four, ag_recv.at[g, zz]).wait()
+            arrived(g, zz)
+            if NEAR_FIRST[n] in (2, 6):
+                relay(g, NEAR_FIRST[n])
             pltpu.make_async_remote_copy(four, four, fw_send.at[g], fw_recv.at[g, zz], {"tok": mate}).start()
             if n % 2 and n >= 5:
                 for zz in order[n - 5 : n - 3]:
@@ -214,29 +237,30 @@
         def _():
             pl.semaphore_signal(go, inc=1, device_id={"tok": t + away * NY * NC})
 
-        for zz in order[4:]:
-            forwarded(zz)
-        for zz in order[4:]:
-            arrange(zz)
+        for pair in (order[4:6], order[6:8]):
+            for zz in pair:
+                forwarded(zz)
+            for zz in pair:
+                arrange(zz)
         for m, ref in enumerate((gt, ut, dt)):
             ref[...] = nat[m, :, 0:HD].astype(BF16)
 
     def gather_drain(g):
-        sends = NY * (LAST_FIRST if g == 0 else NZ - FIRST_SECOND)
-
-        def drain(n):
-            some = ag.at[g, 0, pl.ds(0, n)]
-            pltpu.make_async_copy(some, some, ag_send.at[g]).wait()
+        taking = [z < LAST_FIRST if g == 0 else z >= FIRST_SECOND for z in range(NZ)]
+        weights = ((1, 2 * NY), (7, 2 * NY), (0, NY - 1), (2, NY // 2), (6, NY // 2))
+        sent = [2 * NY + sum(n for dz, n in weights if taking[(z + dz) % NZ]) for z in range(NZ)]
+        for n in sorted(set(sent)):
+            same = functools.reduce(jnp.logical_or, [zme == z for z in range(NZ) if sent[z] == n])
+
+            @pl.when(same)
+            def _():
+                some = ag.at[g, 0, pl.ds(0, n)]
+                pltpu.make_async_copy(some, some, ag_send.at[g]).wait()
 
         @pl.when(live[g])
         def _():
-            drain(sends - 1)
             every = ag.at[g, 0]
             pltpu.make_async_copy(every, every, fw_send.at[g]).wait()
-
-        @pl.when(jnp.logical_not(live[g]))
-        def _():
-            drain(sends)
 
     def grads(g):
         kk, e = k[pl.ds(0, HD)], es[g]
@@ -362,6 +386,7 @@
 
     @pl.when(jnp.logical_not(live[0]))
     def _():
+        relay_only(0)
         pl.semaphore_wait(go, 1)
         far_copy(0).start()
 
@@ -389,6 +414,7 @@
 
     @pl.when(jnp.logical_not(live[1]))
     def _():
+        relay_only(1)
         pl.semaphore_wait(go, 1)
         far_copy(1).start()
 

time: 69.7 us -> 66.5 us (0.954)
  Pallas kernels: 68.3 us -> 65 us
    pallas_call x1, Pallas kernels: 67.5 us -> 64.3 us  [on_device(): pl.pallas_call(kernel, out_shape=shapes, in_specs=[pl.BlockSpec(memory_sp...]
where the time goes in v7:
time: 66.5 us; the launch traced here: 66.3 us
  Pallas kernels  65 us (98%)
  between operations  1.29 us (2%)
    pallas_call x1, Pallas kernels, on_device(): pl.pallas_call(kernel, out_shape=shapes, in_specs=[pl.BlockSpec(memory_sp...  64.3 us

profile of v7, /device:TPU:1, one launch (start us, length us, event | category | flops | bytes accessed | tf_op | source)
XLA Modules:
  0.0 66.3 jit_solution(16358222999736101248)
XLA Ops:
  1.3 64.3 %layer.1 = (bf16[320,256]{1,0:T(8,128)(2,1)S(1)}, f32[5,1,320]{2,1,0:T(1,128)S(1)}, f32[5,1,320]{2,1,0:T(1,128)S(1)}, f32[5,1,320]{2,1,0:T(1,128)S(1)}) custom-call(s32[1]{0:T(128)S(6)} %copy.15.ge, bf16[320,256]{1,0:T(8,128)(2,1)} %bitcast.12, bf16[320,256]{1,0:T(8,128)(2,1)} %bitcast.13, bf16[320,256]{1,0:T(8,128)(2,1)} %bitcast.14, f32[1,256]{1,0:T(1,128)} %bitcast.18, ...), custom_call_target="tpu_custom_call" | custom-call | tf_op jit(solution)/shard_map/layer/pallas_call | solution.py:474
  65.6 0.7 %write_out.1 = (bf16[320,256]{1,0:T(8,128)(2,1)}, f32[5,1,320]{2,1,0:T(1,128)}, f32[5,1,320]{2,1,0:T(1,128)}, f32[5,1,320]{2,1,0:T(1,128)}) custom-call(bf16[320,256]{1,0:T(8,128)(2,1)S(1)} %get-tuple-element.12.refs_0_, f32[5,1,320]{2,1,0:T(1,128)S(1)} %get-tuple-element.13.refs_1_, f32[5,1,320]{2,1,0:T(1,128)S(1)} %get-tuple-element.14.refs_2_, ...), custom_call_target="tpu_custom_call" | custom-call | tf_op jit(solution)/shard_map/write_out/pallas_call | solution.py:529

commit v8 on v7

--- a/solution.py
+++ b/solution.py
@@ -15,6 +15,7 @@
 WINDOW = 512
 NZ, NY, NC = 8, 4, 2
 CHIPS = NZ * NY
+NX = 4
 OWN = 5
 SLOT = 16
 LINES = 40
@@ -114,13 +115,17 @@
 
     barrier = pltpu.get_barrier_semaphore()
 
-    for dz in FAR_FIRST:
+    for dz in (2, 6, 1, 7, 0):
         zz = lax.rem(zme + dz, NZ)
         for dy in range(NY):
             if dz or dy:
                 pl.semaphore_signal(barrier, inc=1, device_id=at_chip(zz * NY + lax.rem(yme + dy, NY)))
-    for n in range(1, HEADS):
-        pl.semaphore_signal(barrier, inc=1, device_id={"head": lax.rem(h + n, HEADS)})
+    across, along = lax.div(h, NX), lax.rem(h, NX)
+    opposite = {"head": (1 - across) * NX + along}
+    pl.semaphore_signal(barrier, inc=1, device_id=opposite)
+    beside = [{"head": across * NX + lax.rem(along + n, NX)} for n in range(1, NX)]
+    for there in beside:
+        pl.semaphore_signal(barrier, inc=1, device_id=there)
     pl.semaphore_signal(barrier, inc=1, device_id={"tok": mate})
     for load in loads:
         load.start()
@@ -140,7 +145,7 @@
     es[1] = (-jnp.where(first, 0.0, rate) * vf).astype(BF16)
     y_buf[...] = jnp.zeros_like(y_buf)
 
-    pl.semaphore_wait(barrier, (CHIPS - 1) + 1 + (HEADS - 1))
+    pl.semaphore_wait(barrier, (5 * NY - 1) + 1 + (NX - 1) + 1)
 
     def active(g, z):
         return z < LAST_FIRST if g == 0 else z >= FIRST_SECOND
@@ -365,10 +370,10 @@
     def exchange_squares():
         mixed = y_buf[...]
         sums = jnp.sum(mixed * mixed, axis=0, keepdims=True)
-        sq[...] = sums
-        sqr[h] = sums
-        for n in range(1, HEADS):
-            pltpu.make_async_remote_copy(sq, sqr.at[h], sq_send, sq_recv, {"head": lax.rem(h + n, HEADS)}).start()
+        sq[0] = sums
+        sqr[along] = sums
+        for there in beside:
+            pltpu.make_async_remote_copy(sq.at[0], sqr.at[along], sq_send.at[0], sq_recv.at[0], there).start()
 
     gather_start(0)
 
@@ -433,19 +438,23 @@
     def _():
         exchange_squares()
 
+    three = sqr.at[pl.ds(0, NX - 1)]
+    pltpu.make_async_copy(three, three, sq_recv.at[0]).wait()
+    sq[1] = jnp.sum(sqr[...], axis=0)
+    squares = pltpu.make_async_remote_copy(sq.at[1], sq.at[2], sq_send.at[1], sq_recv.at[1], opposite)
+    squares.start()
     pass_on(1)
     near_copy(1, v).wait()
     attn = nn(kv_far[1], probs[0]) + nn(kv_near[1], probs[1]) + nn(v[...], probs[2])
-    seven = sqr.at[pl.ds(0, HEADS - 1)]
-    pltpu.make_async_copy(seven, seven, sq_recv).wait()
-    mean_square = jnp.sum(sqr[...], axis=0) / (HEADS * HD)
+    squares.wait()
+    mean_square = (sq[1] + sq[2]) / (HEADS * HD)
     gains = jnp.broadcast_to(gain[...].reshape(1, HD), (8, HD)).T[:, 0:1]
     normed = y_buf[...] / jnp.sqrt(mean_square + 1e-06) * gains
     out[...] = (normed + attn).astype(BF16)
     last = unpack(reduce_finish(1))
     for m, ref in enumerate((g_out, u_out, d_out)):
         ref[...] = last[m * OWN : (m + 1) * OWN].reshape(OWN, 1, HD)
-    pltpu.make_async_copy(seven, seven, sq_send).wait()
+    pltpu.make_async_copy(three, three, sq_send.at[0]).wait()
     for g in range(2):
         gather_drain(g)
         reduce_drain(g)
@@ -493,8 +502,8 @@
             pltpu.VMEM((2, LAST_FIRST * NY, LINES, 128), BF16),
             pltpu.VMEM((2, HD, toks), BF16),
             pltpu.VMEM((2, HD, toks), BF16),
-            pltpu.VMEM((1, toks), F32),
-            pltpu.VMEM((HEADS, 1, toks), F32),
+            pltpu.VMEM((3, 1, toks), F32),
+            pltpu.VMEM((NX, 1, toks), F32),
             pltpu.VMEM((3, HD, PAD), F32),
             pltpu.VMEM((FH, HD), BF16),
             pltpu.VMEM((FH, HD), BF16),
@@ -509,7 +518,7 @@
             dma((2,)), dma((2, NZ)),
             dma((2,)), dma((2,)),
             dma((4,)), dma((4,)),
-            dma, dma,
+            dma((2,)), dma((2,)),
             pltpu.SemaphoreType.REGULAR,
         ],
         compiler_params=pltpu.CompilerParams(

time: 66.5 us -> 65 us (0.977)
  Pallas kernels: 65 us -> 63.5 us
    pallas_call x1, Pallas kernels: 64.3 us -> 62.8 us  [on_device(): pl.pallas_call(kernel, out_shape=shapes, in_specs=[pl.BlockSpec(memory_sp...]
where the time goes in v8:
time: 65 us; the launch traced here: 64.8 us
  Pallas kernels  63.5 us (98%)
  between operations  1.29 us (2%)
    pallas_call x1, Pallas kernels, on_device(): pl.pallas_call(kernel, out_shape=shapes, in_specs=[pl.BlockSpec(memory_sp...  62.8 us

profile of v8, /device:TPU:1, one launch (start us, length us, event | category | flops | bytes accessed | tf_op | source)
XLA Modules:
  0.0 64.8 jit_solution(16314214589280029376)
XLA Ops:
  1.3 62.8 %layer.1 = (bf16[320,256]{1,0:T(8,128)(2,1)S(1)}, f32[5,1,320]{2,1,0:T(1,128)S(1)}, f32[5,1,320]{2,1,0:T(1,128)S(1)}, f32[5,1,320]{2,1,0:T(1,128)S(1)}) custom-call(s32[1]{0:T(128)S(6)} %copy.15.ge, bf16[320,256]{1,0:T(8,128)(2,1)} %bitcast.12, bf16[320,256]{1,0:T(8,128)(2,1)} %bitcast.13, bf16[320,256]{1,0:T(8,128)(2,1)} %bitcast.14, f32[1,256]{1,0:T(1,128)} %bitcast.18, ...), custom_call_target="tpu_custom_call" | custom-call | tf_op jit(solution)/shard_map/layer/pallas_call | solution.py:483
  64.1 0.7 %write_out.1 = (bf16[320,256]{1,0:T(8,128)(2,1)}, f32[5,1,320]{2,1,0:T(1,128)}, f32[5,1,320]{2,1,0:T(1,128)}, f32[5,1,320]{2,1,0:T(1,128)}) custom-call(bf16[320,256]{1,0:T(8,128)(2,1)S(1)} %get-tuple-element.12.refs_0_, f32[5,1,320]{2,1,0:T(1,128)S(1)} %get-tuple-element.13.refs_1_, f32[5,1,320]{2,1,0:T(1,128)S(1)} %get-tuple-element.14.refs_2_, ...), custom_call_target="tpu_custom_call" | custom-call | tf_op jit(solution)/shard_map/write_out/pallas_call | solution.py:538

commit v9 on v8

--- a/solution.py
+++ b/solution.py
@@ -230,10 +230,10 @@
             if NEAR_FIRST[n] in (2, 6):
                 relay(g, NEAR_FIRST[n])
             pltpu.make_async_remote_copy(four, four, fw_send.at[g], fw_recv.at[g, zz], {"tok": mate}).start()
-            if n % 2 and n >= 5:
-                for zz in order[n - 5 : n - 3]:
+            if n >= 6:
+                for zz in order[2 * n - 12 : 2 * n - 10]:
                     forwarded(zz)
-                for zz in order[n - 5 : n - 3]:
+                for zz in order[2 * n - 12 : 2 * n - 10]:
                     arrange(zz)
         far_copy(g).start()
         tell, away = ((2, 3), 4) if g == 0 else ((4, 5), -4)
@@ -242,7 +242,7 @@
         def _():
             pl.semaphore_signal(go, inc=1, device_id={"tok": t + away * NY * NC})
 
-        for pair in (order[4:6], order[6:8]):
+        for pair in (order[4:6], order[6:7], order[7:8]):
             for zz in pair:
                 forwarded(zz)
             for zz in pair:
@@ -319,10 +319,10 @@
             red[g, here] = (gs[g, c, here].astype(F32) + cr[g, here].astype(F32)).astype(BF16)
             peers((dz,), send)
 
-        for half in (FAR_FIRST[: NZ // 2], FAR_FIRST[NZ // 2 :]):
-            for dz in half:
+        for batch in (FAR_FIRST[:2], FAR_FIRST[2:4], FAR_FIRST[4:]):
+            for dz in batch:
                 split(lax.rem(zme + dz, NZ))
-            for dz in half:
+            for dz in batch:
                 to_mate(lax.rem(zme + dz, NZ))
         meanwhile()
         for dz in FAR_FIRST:

time: 65 us -> 64.5 us (level)
  no operation moved by 1% of the time
where the time goes in v9:
time: 64.5 us; the launch traced here: 64.4 us
  Pallas kernels  63.1 us (98%)
  between operations  1.29 us (2%)
    pallas_call x1, Pallas kernels, on_device(): pl.pallas_call(kernel, out_shape=shapes, in_specs=[pl.BlockSpec(memory_sp...  62.4 us

profile of v9, /device:TPU:1, one launch (start us, length us, event | category | flops | bytes accessed | tf_op | source)
XLA Modules:
  0.0 64.4 jit_solution(13480054195151750164)
XLA Ops:
  1.3 62.4 %layer.1 = (bf16[320,256]{1,0:T(8,128)(2,1)S(1)}, f32[5,1,320]{2,1,0:T(1,128)S(1)}, f32[5,1,320]{2,1,0:T(1,128)S(1)}, f32[5,1,320]{2,1,0:T(1,128)S(1)}) custom-call(s32[1]{0:T(128)S(6)} %copy.15.ge, bf16[320,256]{1,0:T(8,128)(2,1)} %bitcast.12, bf16[320,256]{1,0:T(8,128)(2,1)} %bitcast.13, bf16[320,256]{1,0:T(8,128)(2,1)} %bitcast.14, f32[1,256]{1,0:T(1,128)} %bitcast.18, ...), custom_call_target="tpu_custom_call" | custom-call | tf_op jit(solution)/shard_map/layer/pallas_call | solution.py:483
  63.6 0.7 %write_out.1 = (bf16[320,256]{1,0:T(8,128)(2,1)}, f32[5,1,320]{2,1,0:T(1,128)}, f32[5,1,320]{2,1,0:T(1,128)}, f32[5,1,320]{2,1,0:T(1,128)}) custom-call(bf16[320,256]{1,0:T(8,128)(2,1)S(1)} %get-tuple-element.12.refs_0_, f32[5,1,320]{2,1,0:T(1,128)S(1)} %get-tuple-element.13.refs_1_, f32[5,1,320]{2,1,0:T(1,128)S(1)} %get-tuple-element.14.refs_2_, ...), custom_call_target="tpu_custom_call" | custom-call | tf_op jit(solution)/shard_map/write_out/pallas_call | solution.py:538

commit v10 on v9

--- a/solution.py
+++ b/solution.py
@@ -203,6 +203,14 @@
     def block_at(zz):
         return pl.ds(pl.multiple_of(zz * ZROWS, 8), ZROWS)
 
+    def start_far(g):
+        far_copy(g).start()
+        tell, away = ((2, 3), 4) if g == 0 else ((4, 5), -4)
+
+        @pl.when((zme == tell[0]) | (zme == tell[1]))
+        def _():
+            pl.semaphore_signal(go, inc=1, device_id={"tok": t + away * NY * NC})
+
     def gather_finish(g):
         def forwarded(zz):
             four = ag.at[g, 1 - c, pl.ds(zz * NY, NY)]
@@ -225,6 +233,8 @@
 
         order = [lax.rem(zme + dz, NZ) for dz in NEAR_FIRST]
         for n, zz in enumerate(order):
+            if n == NZ - 1:
+                start_far(g)
             four = ag.at[g, c, pl.ds(zz * NY, NY)]
             arrived(g, zz)
             if NEAR_FIRST[n] in (2, 6):
@@ -235,13 +245,6 @@
                     forwarded(zz)
                 for zz in order[2 * n - 12 : 2 * n - 10]:
                     arrange(zz)
-        far_copy(g).start()
-        tell, away = ((2, 3), 4) if g == 0 else ((4, 5), -4)
-
-        @pl.when((zme == tell[0]) | (zme == tell[1]))
-        def _():
-            pl.semaphore_signal(go, inc=1, device_id={"tok": t + away * NY * NC})
-
         for pair in (order[4:6], order[6:7], order[7:8]):
             for zz in pair:
                 forwarded(zz)

time: 64.5 us -> 63.6 us (0.986)
  Pallas kernels: 63.1 us -> 62.1 us
    pallas_call x1, Pallas kernels: 62.4 us -> 61.4 us  [on_device(): pl.pallas_call(kernel, out_shape=shapes, in_specs=[pl.BlockSpec(memory_sp...]
where the time goes in v10:
time: 63.6 us; the launch traced here: 63.4 us
  Pallas kernels  62.1 us (98%)
  between operations  1.29 us (2%)
    pallas_call x1, Pallas kernels, on_device(): pl.pallas_call(kernel, out_shape=shapes, in_specs=[pl.BlockSpec(memory_sp...  61.4 us

profile of v10, /device:TPU:1, one launch (start us, length us, event | category | flops | bytes accessed | tf_op | source)
XLA Modules:
  0.0 63.4 jit_solution(11958260023996433044)
XLA Ops:
  1.3 61.4 %layer.1 = (bf16[320,256]{1,0:T(8,128)(2,1)S(1)}, f32[5,1,320]{2,1,0:T(1,128)S(1)}, f32[5,1,320]{2,1,0:T(1,128)S(1)}, f32[5,1,320]{2,1,0:T(1,128)S(1)}) custom-call(s32[1]{0:T(128)S(6)} %copy.15.ge, bf16[320,256]{1,0:T(8,128)(2,1)} %bitcast.12, bf16[320,256]{1,0:T(8,128)(2,1)} %bitcast.13, bf16[320,256]{1,0:T(8,128)(2,1)} %bitcast.14, f32[1,256]{1,0:T(1,128)} %bitcast.18, ...), custom_call_target="tpu_custom_call" | custom-call | tf_op jit(solution)/shard_map/layer/pallas_call | solution.py:486
  62.7 0.7 %write_out.1 = (bf16[320,256]{1,0:T(8,128)(2,1)}, f32[5,1,320]{2,1,0:T(1,128)}, f32[5,1,320]{2,1,0:T(1,128)}, f32[5,1,320]{2,1,0:T(1,128)}) custom-call(bf16[320,256]{1,0:T(8,128)(2,1)S(1)} %get-tuple-element.12.refs_0_, f32[5,1,320]{2,1,0:T(1,128)S(1)} %get-tuple-element.13.refs_1_, f32[5,1,320]{2,1,0:T(1,128)S(1)} %get-tuple-element.14.refs_2_, ...), custom_call_target="tpu_custom_call" | custom-call | tf_op jit(solution)/shard_map/write_out/pallas_call | solution.py:541
